TPU v7x, 32 devices: a whole 2x2x4 slice. The times are simulated.
32 devices in a mesh: shard: 8 (over z, x), rep: 4 (over y, core).
Axes of the slice: x: 2, y: 2, z: 4, core: 2. Of those that a mesh axis runs over, the one named last changes fastest.
Arguments:
- images: bfloat16 [32, 197, 768], P(('shard', 'rep')), may hold values from -6 to 6
- cotangent: bfloat16 [32, 197, 768], P(('shard', 'rep')), may hold values from -6 to 6
- weights_in: float32 [768, 6144], P('shard'), may hold values from -13 to 13
- weights_down: float32 [3072, 768], P('shard'), may hold values from -0.109375 to 0.109375
- vectors: float32 [12, 768], P(None, 'shard'), may hold values from -1.5 to 1.5, as said below
- mean_in: float32 [768, 6144], P('shard'), may hold values from -256 to 256
- mean_down: float32 [3072, 768], P('shard'), may hold values from -256 to 256
- mean_vectors: float32 [12, 768], P(None, 'shard'), may hold values from -256 to 256
- square_in: float32 [768, 6144], P('shard'), may hold values from 63.04 to 6304
- square_down: float32 [3072, 768], P('shard'), may hold values from 63.04 to 6304
- square_vectors: float32 [12, 768], P(None, 'shard'), may hold values from 63.04 to 6304
Outputs:
- block_out: bfloat16 [32, 197, 768], P(('shard', 'rep'))
- input_grad: float32 [32, 197, 768], P(('shard', 'rep'))
- grad_in: float32 [768, 6144], P('shard')
- grad_down: float32 [3072, 768], P('shard')
- grad_vectors: float32 [12, 768], P(None, 'shard')
- updated_in: float32 [768, 6144], P('shard')
- updated_down: float32 [3072, 768], P('shard')
- updated_vectors: float32 [12, 768], P(None, 'shard')
- next_mean_in: float32 [768, 6144], P('shard')
- next_mean_down: float32 [3072, 768], P('shard')
- next_mean_vectors: float32 [12, 768], P(None, 'shard')
- next_square_in: float32 [768, 6144], P('shard')
- next_square_down: float32 [3072, 768], P('shard')
- next_square_vectors: float32 [12, 768], P(None, 'shard')
Inputs may be any that keep to these rules, and one draw needn't show every extreme that they name: `vectors`: rows 0 and 5 are the norms' gains.
All inputs are finite; a program needn't handle non-finite values.
Results may differ from a plain program's by a relative error of at most 0.023.
Values may be sent and summed in bfloat16 or wider, within the bound.
A program may use at most 128 MiB of HBM per device.

v0:
```python
import math

import jax
import jax.numpy as jnp
from jax import lax
from jax.sharding import PartitionSpec as P

HEADS = 12


NORM_EPS = 1e-06
BETA_ONE = 0.9
BETA_TWO = 0.95
ADAM_EPS = 1e-08
RATE_MATRIX = 0.008
RATE_VECTOR = 0.15
DECAY_MATRIX = 0.05
STEP_COUNT = 2.0


def to_half(array_in):
    return array_in.astype(jnp.bfloat16)


def matmul(left, right):
    return jnp.dot(left, right, preferred_element_type=jnp.float32)


def times_transposed(left, right):
    return lax.dot_general(
        left, right, (((1,), (1,)), ((), ())), preferred_element_type=jnp.float32
    )


def transposed_times(left, right):
    return lax.dot_general(
        left, right, (((0,), (0,)), ((), ())), preferred_element_type=jnp.float32
    )


def layer_norm(inputs, gain, shift):
    centred = inputs - jnp.mean(inputs, axis=-1, keepdims=True)
    inv_std = lax.rsqrt(jnp.mean(centred * centred, axis=-1, keepdims=True) + NORM_EPS)
    normed = centred * inv_std
    return (normed, inv_std, normed * gain + shift)


def norm_back(grad_after, normed, inv_std, gain):
    grad_normed = grad_after * gain
    grad_inputs = inv_std * (
        grad_normed
        - jnp.mean(grad_normed, axis=-1, keepdims=True)
        - normed * jnp.mean(grad_normed * normed, axis=-1, keepdims=True)
    )
    return (grad_inputs, jnp.sum(grad_after * normed, axis=0), jnp.sum(grad_after, axis=0))


def gaussian_unit(hidden):
    cdf_part = 0.5 * (1.0 + jax.scipy.special.erf(hidden * 0.7071067811865476))
    slope = cdf_part + hidden * jnp.exp(-0.5 * hidden * hidden) * 0.3989422804014327
    return (hidden * cdf_part, slope)


def head_scores(query_heads, key_heads, score_scale):
    return (
        jnp.einsum("bqhe,bkhe->bhqk", query_heads, key_heads, preferred_element_type=jnp.float32)
        * score_scale
    )


def forward_pass(images, matrix_half, down_half, vector_half):
    img_count, seq_len, model_width = images.shape
    head_dim = model_width // HEADS
    score_scale = 1.0 / math.sqrt(head_dim)
    row_count = img_count * seq_len
    head_shape = (img_count, seq_len, HEADS, head_dim)
    vector_float = vector_half.astype(jnp.float32)
    flat_in = images.reshape(row_count, model_width).astype(jnp.float32)
    normed_one, inv_one, pre_one = layer_norm(flat_in, vector_float[0], vector_float[1])
    act_one = to_half(pre_one)
    projected = matmul(act_one, matrix_half[:, : 3 * model_width])
    query_heads = to_half(projected[:, :model_width] + vector_float[2]).reshape(head_shape)
    key_heads = to_half(projected[:, model_width : 2 * model_width]).reshape(head_shape)
    value_heads = to_half(projected[:, 2 * model_width :] + vector_float[3]).reshape(head_shape)
    scores = head_scores(query_heads, key_heads, score_scale)
    log_total = jax.nn.logsumexp(scores, axis=-1, keepdims=True)
    probs_half = to_half(jnp.exp(scores - log_total))
    attended = to_half(
        jnp.einsum(
            "bhqk,bkhe->bqhe", probs_half, value_heads, preferred_element_type=jnp.float32
        ).reshape(row_count, model_width)
    )
    hidden_one = (
        flat_in
        + matmul(attended, matrix_half[:, 3 * model_width : 4 * model_width])
        + vector_float[4]
    )
    normed_two, inv_two, pre_two = layer_norm(hidden_one, vector_float[5], vector_float[6])
    act_two = to_half(pre_two)
    up_input = matmul(act_two, matrix_half[:, 4 * model_width :]) + vector_float[8:].reshape(-1)
    gelu_out, gelu_slope = gaussian_unit(up_input)
    gelu_half = to_half(gelu_out)
    block_out = to_half(hidden_one + matmul(gelu_half, down_half) + vector_float[7])
    saved = (
        normed_one,
        inv_one,
        act_one,
        query_heads,
        key_heads,
        value_heads,
        log_total,
        attended,
        normed_two,
        inv_two,
        act_two,
        gelu_slope,
        gelu_half,
    )
    return (block_out.reshape(images.shape), saved)


def backward_pass(cotangent, saved, matrix_half, down_half, vector_half):
    (
        normed_one,
        inv_one,
        act_one,
        query_heads,
        key_heads,
        value_heads,
        log_total,
        attended,
        normed_two,
        inv_two,
        act_two,
        gelu_slope,
        gelu_half,
    ) = saved
    img_count, seq_len, model_width = cotangent.shape
    head_dim = model_width // HEADS
    score_scale = 1.0 / math.sqrt(head_dim)
    row_count = img_count * seq_len
    head_shape = (img_count, seq_len, HEADS, head_dim)
    vector_float = vector_half.astype(jnp.float32)
    joint_weights = matrix_half[:, : 3 * model_width]
    output_weights = matrix_half[:, 3 * model_width : 4 * model_width]
    upward_weights = matrix_half[:, 4 * model_width :]
    grad_half = cotangent.reshape(row_count, model_width)
    grad_out = grad_half.astype(jnp.float32)
    grad_up = times_transposed(grad_half, down_half) * gelu_slope
    up_half = to_half(grad_up)
    grad_act_two = times_transposed(up_half, upward_weights)
    grad_norm_two, grad_gain_two, grad_shift_two = norm_back(
        grad_act_two, normed_two, inv_two, vector_float[5]
    )
    grad_hidden = grad_out + grad_norm_two
    hidden_half = to_half(grad_hidden)
    grad_att = to_half(times_transposed(hidden_half, output_weights)).reshape(head_shape)
    prob_float = jnp.exp(head_scores(query_heads, key_heads, score_scale) - log_total)
    probs_half = to_half(prob_float)
    grad_probs = jnp.einsum(
        "bqhe,bkhe->bhqk", grad_att, value_heads, preferred_element_type=jnp.float32
    )
    row_inner = jnp.sum(prob_float * grad_probs, axis=-1, keepdims=True)
    grad_scores = to_half(prob_float * (grad_probs - row_inner) * score_scale)
    grad_query = jnp.einsum(
        "bhqk,bkhe->bqhe", grad_scores, key_heads, preferred_element_type=jnp.float32
    ).reshape(row_count, model_width)
    grad_key = jnp.einsum(
        "bhqk,bqhe->bkhe", grad_scores, query_heads, preferred_element_type=jnp.float32
    ).reshape(row_count, model_width)
    grad_value = jnp.einsum(
        "bhqk,bqhe->bkhe", probs_half, grad_att, preferred_element_type=jnp.float32
    ).reshape(row_count, model_width)
    grad_proj = to_half(jnp.concatenate([grad_query, grad_key, grad_value], axis=1))
    grad_act_one = times_transposed(grad_proj, joint_weights)
    grad_norm_one, grad_gain_one, grad_shift_one = norm_back(
        grad_act_one, normed_one, inv_one, vector_float[0]
    )
    input_grad = (grad_hidden + grad_norm_one).reshape(cotangent.shape)
    grad_down = transposed_times(gelu_half, grad_half)
    small_rows = jnp.stack(
        [
            grad_gain_one,
            grad_shift_one,
            jnp.sum(grad_query, axis=0),
            jnp.sum(grad_value, axis=0),
            jnp.sum(grad_hidden, axis=0),
            grad_gain_two,
            grad_shift_two,
            jnp.sum(grad_out, axis=0),
        ]
    )
    grad_vectors = jnp.concatenate(
        [small_rows, jnp.sum(grad_up, axis=0).reshape(4, model_width)], axis=0
    )
    factors = (act_one, grad_proj, attended, hidden_half, act_two, up_half)
    return (input_grad, grad_down, grad_vectors, factors)


def adam_update(weights, first, second, gradient, rate, decay):
    next_first = BETA_ONE * first + (1.0 - BETA_ONE) * gradient
    next_second = BETA_TWO * second + (1.0 - BETA_TWO) * gradient * gradient
    corr_first = next_first / (1.0 - BETA_ONE**STEP_COUNT)
    corr_second = next_second / (1.0 - BETA_TWO**STEP_COUNT)
    updated = weights - rate * (corr_first / (jnp.sqrt(corr_second) + ADAM_EPS) + decay * weights)
    return (updated, next_first, next_second)


def local(
    images,
    cotangent,
    weights_in,
    weights_down,
    vectors,
    mean_in,
    mean_down,
    mean_vectors,
    square_in,
    square_down,
    square_vectors,
):
    halves = (to_half(weights_in), to_half(weights_down), to_half(vectors))
    forward_set = (
        lax.all_gather(halves[0], "shard", axis=0, tiled=True),
        lax.all_gather(halves[1], "shard", axis=0, tiled=True),
        lax.all_gather(halves[2], "shard", axis=1, tiled=True),
    )
    block_out, saved = forward_pass(images, forward_set[0], forward_set[1], forward_set[2])
    backward_set = (
        lax.all_gather(halves[0], "shard", axis=0, tiled=True),
        lax.all_gather(halves[1], "shard", axis=0, tiled=True),
        lax.all_gather(halves[2], "shard", axis=1, tiled=True),
    )
    input_grad, grad_down_local, grad_vectors_local, factors = backward_pass(
        cotangent, saved, backward_set[0], backward_set[1], backward_set[2]
    )
    act_one, grad_proj, attended, hidden_half, act_two, up_half = factors

    def column_part(activation, gradient):
        return transposed_times(activation, gradient)

    owned_in = lax.psum_scatter(
        jnp.concatenate(
            [
                column_part(act_one, grad_proj),
                column_part(attended, hidden_half),
                column_part(act_two, up_half),
            ],
            axis=1,
        ).astype(jnp.bfloat16),
        "shard",
        scatter_dimension=0,
        tiled=True,
    )
    owned_down, owned_vectors = (
        lax.psum_scatter(
            grad_down_local.astype(jnp.bfloat16), "shard", scatter_dimension=0, tiled=True
        ).astype(jnp.float32),
        lax.psum_scatter(
            grad_vectors_local.astype(jnp.bfloat16), "shard", scatter_dimension=1, tiled=True
        ).astype(jnp.float32),
    )
    grad_in, grad_down, grad_vectors = (
        lax.psum(owned_in, "rep").astype(jnp.float32),
        lax.psum(owned_down.astype(jnp.bfloat16), "rep").astype(jnp.float32),
        lax.psum(owned_vectors.astype(jnp.bfloat16), "rep").astype(jnp.float32),
    )
    new_in = adam_update(weights_in, mean_in, square_in, grad_in, RATE_MATRIX, DECAY_MATRIX)
    new_down = adam_update(
        weights_down, mean_down, square_down, grad_down, RATE_MATRIX, DECAY_MATRIX
    )
    new_vectors = adam_update(vectors, mean_vectors, square_vectors, grad_vectors, RATE_VECTOR, 0.0)
    return (
        block_out,
        input_grad,
        grad_in,
        grad_down,
        grad_vectors,
        new_in[0],
        new_down[0],
        new_vectors[0],
        new_in[1],
        new_down[1],
        new_vectors[1],
        new_in[2],
        new_down[2],
        new_vectors[2],
    )


def solution(mesh):
    placed = (
        P(("shard", "rep"), None, None),
        P(("shard", "rep"), None, None),
        P("shard", None),
        P("shard", None),
        P(None, "shard"),
        P("shard", None),
        P("shard", None),
        P(None, "shard"),
        P("shard", None),
        P("shard", None),
        P(None, "shard"),
    )
    return jax.shard_map(
        local,
        mesh=mesh,
        in_specs=placed,
        out_specs=(
            P(("shard", "rep"), None, None),
            P(("shard", "rep"), None, None),
            P("shard", None),
            P("shard", None),
            P(None, "shard"),
            P("shard", None),
            P("shard", None),
            P(None, "shard"),
            P("shard", None),
            P("shard", None),
            P(None, "shard"),
            P("shard", None),
            P("shard", None),
            P(None, "shard"),
        ),
        check_vma=False,
    )
```

profile of v0, /device:TPU:0, one launch (start us, length us, event | category | flops | bytes accessed | tf_op | source)
XLA Modules:
  0.0 623.4 jit_solution(6696602671923517766)
XLA Ops:
  7.2 2.9 convert_element_type.95
  11.2 33.3 %all-gather = bf16[8,96,12]{1,2,0:T(8,128)(2,1)S(1)} all-gather(bf16[1,96,12]{1,2,0:T(8,128)(2,1)S(1)} %convert_bitcast_fusion.1), channel_id=1, replica_groups=mesh['shard'=8,'rep'=4] {'shard'}, dimensions={0}, use_global_device_ids=true | all-gather | bytes 20736 | tf_op jit(solution)/shard_map/all_gather | solution.py:226
  45.1 105.8 %all-gather.4.cloned.1.call-done = bf16[768,6144]{1,0:T(8,128)(2,1)} async-done(((bf16[96,6144]{1,0:T(8,128)(2,1)}), bf16[768,6144]{1,0:T(8,128)(2,1)}) %all-gather.4.cloned.1.call-update) | async-done | bytes 9437200 | tf_op jit(solution)/shard_map/all_gather | solution.py:224
  150.9 3.0 fusion.10
  160.3 5.4 multiply_convert_fusion.1
  166.7 3.7 convolution_convert_fusion
  170.7 60.5 %all-gather.6.cloned.1.call-done = bf16[3072,768]{1,0:T(8,128)(2,1)} async-done(((bf16[384,768]{1,0:T(8,128)(2,1)}), bf16[3072,768]{1,0:T(8,128)(2,1)}) %all-gather.6.cloned.1.call-update) | async-done | bytes 4718608 | tf_op jit(solution)/shard_map/all_gather | solution.py:225
  231.2 5.0 fusion.90
  236.2 4.7 multiply_reduce_fusion.2
  242.3 2.5 convolution_convert_fusion.5
  246.7 2.5 convolution_convert_fusion.3
  251.6 3.0 fusion.91
  254.6 4.7 fusion.30
  259.3 4.9 fusion.86
  268.7 4.2 pad_maximum_fusion
  274.3 3.6 fusion.56
  278.9 50.0 %reduce-scatter.8.cloned.1.call-done = bf16[384,768]{1,0:T(8,128)(2,1)} async-done(((bf16[3072,768]{1,0:T(8,128)(2,1)}), bf16[384,768]{1,0:T(8,128)(2,1)}) %reduce-scatter.8.cloned.1.call-update) | async-done | bytes 589840 | tf_op jit(solution)/shard_map/reduce_scatter | solution.py:256
  328.9 165.2 %reduce-scatter.6.cloned.1.call-done = bf16[96,6144]{1,0:T(8,128)(2,1)} async-done(((bf16[768,6144]{1,0:T(8,128)(2,1)}), bf16[96,6144]{1,0:T(8,128)(2,1)}) %reduce-scatter.6.cloned.1.call-update) | async-done | bytes 1179664 | tf_op jit(solution)/shard_map/reduce_scatter | solution.py:242
  495.9 4.3 fusion.37
  500.2 58.6 %reduce-scatter.10.cloned.1.call-done = bf16[96,12]{1,0:T(8,128)(2,1)} async-done(((bf16[768,12]{1,0:T(8,128)(2,1)}), bf16[96,12]{1,0:T(8,128)(2,1)}) %reduce-scatter.10.cloned.1.call-update) | async-done | bytes 2320
  559.6 5.7 psum.23
  565.9 40.4 %all-reduce.3.cloned.1.call-done = (bf16[96,6144]{1,0:T(8,128)(2,1)}, bf16[384,768]{1,0:T(8,128)(2,1)}) async-done(((bf16[96,6144]{1,0:T(8,128)(2,1)}, bf16[384,768]{1,0:T(8,128)(2,1)}), (bf16[96,6144]{1,0:T(8,128)(2,1)}, bf16[384,768]{1,0:T(8,128)(2,1)})) %all-reduce.3.cloned.1.call-update) | async-done | bytes 1769488 | tf_op jit(solution)/shard_map/psum | solution.py:264
  606.3 4.6 multiply_subtract_fusion.1
  612.3 4.3 multiply_subtract_fusion
  (126 shorter events, 26.2 us)
Async XLA Ops:
  7.2 3.0 copy-start.3
  7.2 143.7 %all-gather.4.cloned.1.call-start = ((), (), s32[]{:S(2)}) async-start(), calls=%async_computation.3 | async-start | bytes 10616832 | tf_op jit(solution)/shard_map/all_gather | solution.py:224
  10.1 34.5 %copy-start.9 = (bf16[1,197,768]{2,1,0:T(8,128)(2,1)S(1)}, bf16[1,197,768]{2,1,0:T(8,128)(2,1)}, u32[]{:S(2)}) copy-start(bf16[1,197,768]{2,1,0:T(8,128)(2,1)} %param.11) | copy-start | bytes 907780
  10.2 221.0 %all-gather.6.cloned.1.call-start = ((), (), s32[]{:S(2)}) async-start(), calls=%async_computation.4 | async-start | bytes 5308416 | tf_op jit(solution)/shard_map/all_gather | solution.py:225
  11.1 317.8 %reduce-scatter.8.cloned.1.call-start = ((), (), s32[]{:S(2)}) async-start(), calls=%async_computation.6 | async-start | bytes 5308416 | tf_op jit(solution)/shard_map/reduce_scatter | solution.py:256
  155.1 2.2 copy-start.18
  158.0 2.3 copy-start.19
  160.0 76.2 %copy-start.1 = (f32[197,768]{1,0:T(8,128)}, f32[197,768]{1,0:T(8,128)S(1)}, u32[]{:S(2)}) copy-start(f32[197,768]{1,0:T(8,128)S(1)} %get-tuple-element.111) | copy-start | bytes 1815556
  160.3 6.4 %copy-start.13 = (bf16[1,197,768]{2,1,0:T(8,128)(2,1)S(1)}, bf16[1,197,768]{2,1,0:T(8,128)(2,1)}, u32[]{:S(2)}) copy-start(bf16[1,197,768]{2,1,0:T(8,128)(2,1)} %param.12) | copy-start | bytes 907780
  170.4 323.7 %reduce-scatter.6.cloned.1.call-start = ((), (), s32[]{:S(2)}) async-start(), calls=%async_computation.5 | async-start | bytes 10616832 | tf_op jit(solution)/shard_map/reduce_scatter | solution.py:242
  236.2 4.7 copy-start.20
  236.2 4.7 copy-start.14
  259.3 4.9 copy-start.6
  267.1 1.6 copy-start.5
  272.9 285.9 %reduce-scatter.10.cloned.1.call-start = ((), (), s32[]{:S(2)}) async-start(), calls=%async_computation.7 | async-start | bytes 221184
  278.9 327.5 %all-reduce.3.cloned.1.call-start = ((), (), s32[]{:S(2)}) async-start(), calls=%async_computation.8 | async-start | bytes 3538944 | tf_op jit(solution)/shard_map/psum | solution.py:264
  494.2 1.7 copy-start.8
  495.9 69.4 %copy-start.26 = (f32[12,96]{1,0:T(8,128)S(1)}, f32[12,96]{1,0:T(8,128)}, u32[]{:S(2)}) copy-start(f32[12,96]{1,0:T(8,128)} %param.18) | copy-start | bytes 13828
  495.9 69.4 %copy-start.27 = (f32[12,96]{1,0:T(8,128)S(1)}, f32[12,96]{1,0:T(8,128)}, u32[]{:S(2)}) copy-start(f32[12,96]{1,0:T(8,128)} %param.21) | copy-start | bytes 13828
  495.9 110.4 %copy-start.4 = (f32[384,768]{1,0:T(8,128)S(1)}, f32[384,768]{1,0:T(8,128)}, u32[]{:S(2)}) copy-start(f32[384,768]{1,0:T(8,128)} %param.14) | copy-start | bytes 3538948
  606.3 4.6 copy-start
  606.3 4.6 copy-start.16
  606.3 5.7 copy-start.17
  606.3 5.9 copy-start.22
  (14 other events, 17.4 us)
Sparse Core Ops, SparseCore 0:
  10.8 140.0 all-gather.3
  153.6 77.5 all-gather.5
  234.9 94.0 reduce-scatter.7
  332.3 161.7 reduce-scatter.5
  497.8 60.9 reduce-scatter.9
  561.2 45.0 all-reduce.2
where the time goes:
time: 624 us; the launch traced here: 623 us
  waiting for transfers between devices  481 us (77%)
  matrix products  54.9 us (9%)
  blocking collectives  38.9 us (6%)
  other arithmetic  20.4 us (3%)
  between operations  14.6 us (2%)
  local copies, waits for them, and re-layouts  13.3 us (2%)
    reduce_scatter x1, waiting for transfers between devices, local(): lax.psum_scatter(jnp.concatenate([column_part(act_one, grad_proj), column...  165 us
    all_gather x1, waiting for transfers between devices, local(): lax.all_gather(halves[0], 'shard', axis=0, tiled=True)  106 us
    all_gather x1, waiting for transfers between devices, local(): lax.all_gather(halves[1], 'shard', axis=0, tiled=True)  60.5 us
    unnamed x7, waiting for transfers between devices  58.7 us
    reduce_scatter x1, waiting for transfers between devices, local(): lax.psum_scatter(grad_down_local.astype(jnp.bfloat16), 'shard', scatter_d...  50 us
    psum x1, waiting for transfers between devices, local(): lax.psum(owned_in, 'rep').astype(jnp.float32)  40.4 us
    all_gather x1, blocking collectives, local(): lax.all_gather(halves[2], 'shard', axis=1, tiled=True)  33.3 us
    dot_general x4, matrix products, times_transposed(): lax.dot_general(left, right, (((1,), (1,)), ((), ())), preferred_element_...  15.7 us
  transfers between devices with their start and end apart: 6, of which 6 were waited for; matrix products, arithmetic and copies ran while one was open for 12% of the time, Pallas kernels for 0%

commit v1 on v0

--- a/solution.py
+++ b/solution.py
@@ -1,8 +1,11 @@
+import functools
 import math
 
 import jax
 import jax.numpy as jnp
 from jax import lax
+from jax.experimental import pallas as pl
+from jax.experimental.pallas import tpu as pltpu
 from jax.sharding import PartitionSpec as P
 
 HEADS = 12
@@ -206,7 +209,281 @@
     return (updated, next_first, next_second)
 
 
+def grid_sizes(shards, reps):
+    x_size = 1
+    while 2 * (2 * x_size) ** 2 <= shards and shards % (2 * x_size) == 0:
+        x_size *= 2
+    core_size = 2 if reps % 2 == 0 else 1
+    return (shards // x_size, x_size, reps // core_size, core_size)
+
+
+def gather_body(
+    sizes, win, wdn, vec, gin, gdn, gvec, local_sem, vec_s, vec_r, *sems
+):
+    nz, nx, ny, nc = sizes
+    shards, reps = nz * nx, ny * nc
+    s = lax.axis_index("shard")
+    r = lax.axis_index("rep")
+    z, x = s // nx, s % nx
+    y, c = r // nc, r % nc
+    width = win.shape[1] // reps
+
+    def shard_of(kz, kx):
+        return lax.rem(z + nz - kz, nz) * nx + lax.rem(x + nx - kx, nx)
+
+    def rep_of(ky):
+        return lax.rem(y + ny - ky, ny) * nc + c
+
+    barrier = pltpu.get_barrier_semaphore()
+    peers = [(lax.rem(s + k, shards), r) for k in range(1, shards)]
+    peers += [(s, lax.rem(y + k, ny) * nc + c) for k in range(1, ny)]
+    peers += [(s, y * nc + lax.rem(c + k, nc)) for k in range(1, nc)]
+    for ps, pr in peers:
+        pl.semaphore_signal(
+            barrier,
+            inc=1,
+            device_id={"shard": ps, "rep": pr},
+            device_id_type=pl.DeviceIdType.MESH,
+        )
+    pl.semaphore_wait(barrier, len(peers))
+
+    started = []
+
+    def send(src, dst, ssem, rsem, ps, pr):
+        copy = pltpu.make_async_remote_copy(
+            src_ref=src,
+            dst_ref=dst,
+            send_sem=ssem,
+            recv_sem=rsem,
+            device_id={"shard": ps, "rep": pr},
+            device_id_type=pl.DeviceIdType.MESH,
+        )
+        copy.start()
+        started.append(copy)
+        return copy
+
+    def in_slot(kz, kx, ky):
+        cols = pl.ds(pl.multiple_of(rep_of(ky) * width, 128), width)
+        return gin.at[shard_of(kz, kx), :, cols]
+
+    def dn_slot(kz, kx, ky):
+        return gdn.at[shard_of(kz, kx), rep_of(ky)]
+
+    own_cols = pl.ds(pl.multiple_of(r * width, 128), width)
+    (zs_i, zr_i, xs_i, xr_i, ys_i, yr_i, cs_i, cr_i) = sems[:8]
+    (zs_d, zr_d, xs_d, xr_d, ys_d, yr_d, cs_d, cr_d) = sems[8:]
+    mine = [
+        pltpu.make_async_copy(win, gin.at[s], local_sem.at[0]),
+        pltpu.make_async_copy(wdn, gdn.at[s], local_sem.at[1]),
+        pltpu.make_async_copy(vec, gvec.at[s], local_sem.at[2]),
+    ]
+    vec_copies = [
+        send(vec, gvec.at[s], vec_s.at[k], vec_r.at[k], lax.rem(s + k, shards), r)
+        for k in range(1, shards)
+    ]
+    zi, zd = {}, {}
+    for k in range(1, nz):
+        peer = lax.rem(z + k, nz) * nx + x
+        zi[k] = send(
+            win.at[:, own_cols], gin.at[s, :, own_cols], zs_i.at[k], zr_i.at[k], peer, r
+        )
+        zd[k] = send(wdn.at[r], gdn.at[s, r], zs_d.at[k], zr_d.at[k], peer, r)
+    xi, xd, yi, yd, ci, cd = {}, {}, {}, {}, {}, {}
+
+    def send_x_in(kz):
+        for kx in range(1, nx):
+            peer = z * nx + lax.rem(x + kx, nx)
+            src = win.at[:, own_cols] if kz == 0 else in_slot(kz, 0, 0)
+            xi[kz, kx] = send(
+                src, in_slot(kz, 0, 0), xs_i.at[kz, kx], xr_i.at[kz, kx], peer, r
+            )
+
+    def send_y_in(kz, kx):
+        for ky in range(1, ny):
+            peer = lax.rem(y + ky, ny) * nc + c
+            slot = in_slot(kz, kx, 0)
+            yi[kz, kx, ky] = send(
+                slot, slot, ys_i.at[kz, kx, ky], yr_i.at[kz, kx, ky], s, peer
+            )
+
+    def send_c_in(kz, kx, ky):
+        if nc > 1:
+            slot = in_slot(kz, kx, ky)
+            ci[kz, kx, ky] = send(
+                slot, slot, cs_i.at[kz, kx, ky], cr_i.at[kz, kx, ky], s, y * nc + 1 - c
+            )
+
+    def send_y_dn(kz):
+        for ky in range(1, ny):
+            peer = lax.rem(y + ky, ny) * nc + c
+            slot = dn_slot(kz, 0, 0)
+            yd[kz, ky] = send(slot, slot, ys_d.at[kz, ky], yr_d.at[kz, ky], s, peer)
+
+    def send_x_dn(kz, ky):
+        for kx in range(1, nx):
+            peer = z * nx + lax.rem(x + kx, nx)
+            src = wdn.at[rep_of(ky)] if kz == 0 else dn_slot(kz, 0, ky)
+            xd[kz, kx, ky] = send(
+                src,
+                dn_slot(kz, 0, ky),
+                xs_d.at[kz, kx, ky],
+                xr_d.at[kz, kx, ky],
+                peer,
+                r,
+            )
+
+    def send_c_dn(kz, kx, ky):
+        if nc > 1:
+            slot = dn_slot(kz, kx, ky)
+            cd[kz, kx, ky] = send(
+                slot, slot, cs_d.at[kz, kx, ky], cr_d.at[kz, kx, ky], s, y * nc + 1 - c
+            )
+
+    send_x_in(0)
+    for ky in range(ny):
+        send_x_dn(0, ky)
+    for copy in mine:
+        copy.start()
+    for kz in range(nz):
+        if kz > 0:
+            zi[kz].wait_recv()
+            send_y_in(kz, 0)
+            send_x_in(kz)
+            send_c_in(kz, 0, 0)
+            zd[kz].wait_recv()
+            send_x_dn(kz, 0)
+            send_y_dn(kz)
+            send_c_dn(kz, 0, 0)
+        for kx in range(1, nx):
+            xi[kz, kx].wait_recv()
+            send_y_in(kz, kx)
+            send_c_in(kz, kx, 0)
+        if kz > 0:
+            for ky in range(1, ny):
+                yd[kz, ky].wait_recv()
+                send_x_dn(kz, ky)
+                send_c_dn(kz, 0, ky)
+    for kz in range(nz):
+        for kx in range(nx):
+            for ky in range(ny):
+                if kx > 0:
+                    xd[kz, kx, ky].wait_recv()
+                    send_c_dn(kz, kx, ky)
+                if ky > 0 and (kz > 0 or kx > 0):
+                    yi[kz, kx, ky].wait_recv()
+                    send_c_in(kz, kx, ky)
+    for copy in list(ci.values()) + list(cd.values()) + vec_copies:
+        copy.wait_recv()
+    for copy in mine:
+        copy.wait()
+    for copy in started:
+        copy.wait_send()
+
+
+def gather_weights(sizes, win, wdn, vec):
+    nz, nx, ny, nc = sizes
+    shards, reps = nz * nx, ny * nc
+    rows_in, cols_in = win.shape
+    rows_dn, cols_dn = wdn.shape
+    dma = pltpu.SemaphoreType.DMA
+    full = (nz, nx, ny)
+    shapes_in = [(nz,), (nz, nx), full, full]
+    shapes_dn = [(nz,), full, (nz, ny), full]
+    sems = [dma(shape) for shape in shapes_in + shapes_dn for _ in range(2)]
+
+    def body(*refs):
+        gather_body(sizes, *refs)
+
+    gin, gdn, gvec = pl.pallas_call(
+        body,
+        name="gather_weights",
+        out_shape=(
+            jax.ShapeDtypeStruct((shards, rows_in, cols_in), win.dtype),
+            jax.ShapeDtypeStruct((shards, reps, rows_dn // reps, cols_dn), wdn.dtype),
+            jax.ShapeDtypeStruct((shards,) + vec.shape, vec.dtype),
+        ),
+        in_specs=[pl.BlockSpec(memory_space=pltpu.VMEM)] * 3,
+        out_specs=[pl.BlockSpec(memory_space=pl.ANY)] * 3,
+        scratch_shapes=[dma((3,)), dma((shards,)), dma((shards,))] + sems,
+        compiler_params=pltpu.CompilerParams(
+            collective_id=0, has_side_effects=True, vmem_limit_bytes=16 << 20
+        ),
+    )(win, wdn.reshape(reps, rows_dn // reps, cols_dn), vec)
+    return (
+        gin.reshape(shards * rows_in, cols_in),
+        gdn.reshape(shards * rows_dn, cols_dn),
+        jnp.swapaxes(gvec, 0, 1).reshape(vec.shape[0], -1),
+    )
+
+
+def axis_info(sizes, name):
+    nz, nx, ny, nc = sizes
+    s = lax.axis_index("shard")
+    r = lax.axis_index("rep")
+    position = {"z": 0, "x": 1, "y": 2, "c": 3}[name]
+    coordinate = (s // nx, s % nx, r // nc, r % nc)[position]
+    size = sizes[position]
+
+    def shift(k):
+        pairs = []
+        for index in range(nz * nx * ny * nc):
+            parts = [
+                index // (nc * ny * nx),
+                index // (nc * ny) % nx,
+                index // nc % ny,
+                index % nc,
+            ]
+            parts[position] = (parts[position] + k) % size
+            target = ((parts[0] * nx + parts[1]) * ny + parts[2]) * nc + parts[3]
+            pairs.append((index, target))
+        return pairs
+
+    return (size, coordinate, shift)
+
+
+def scatter_axis(sizes, value, name, dim):
+    size, me, shift = axis_info(sizes, name)
+    take = lambda i: lax.dynamic_index_in_dim(value, i, dim, keepdims=False)
+    total = take(me).astype(jnp.float32)
+    for k in range(1, size):
+        got = lax.ppermute(take(lax.rem(me + k, size)), ("shard", "rep"), shift(k))
+        total = total + got.astype(jnp.float32)
+    return to_half(total)
+
+
+def reduce_matrix(sizes, partial, order):
+    nz, nx, ny, nc = sizes
+    rows, cols = partial.shape
+    unit = rows // (nz * nx * ny * nc)
+    names = ["z", "x", "y", "c"]
+    value = partial.reshape(nz, nx, ny, nc, unit, cols)
+    for name in order:
+        dim = names.index(name)
+        names.pop(dim)
+        value = scatter_axis(sizes, value, name, dim)
+    reps = ny * nc
+    r = lax.axis_index("rep")
+    whole = jnp.zeros((reps, unit, cols), value.dtype)
+    whole = lax.dynamic_update_index_in_dim(whole, value, r, 0)
+    for k in range(1, reps):
+        got = lax.ppermute(value, "rep", [(i, (i + k) % reps) for i in range(reps)])
+        whole = lax.dynamic_update_index_in_dim(whole, got, lax.rem(r + reps - k, reps), 0)
+    return whole.reshape(reps * unit, cols).astype(jnp.float32)
+
+
+def reduce_small(count, value):
+    if count & (count - 1):
+        return lax.psum(value, ("shard", "rep"))
+    step = 1
+    while step < count:
+        pairs = [(i, i ^ step) for i in range(count)]
+        value = value + lax.ppermute(value, ("shard", "rep"), pairs)
+        step *= 2
+    return value
+
+
 def local(
+    sizes,
     images,
     cotangent,
     weights_in,
@@ -220,50 +497,37 @@
     square_vectors,
 ):
     halves = (to_half(weights_in), to_half(weights_down), to_half(vectors))
-    forward_set = (
-        lax.all_gather(halves[0], "shard", axis=0, tiled=True),
-        lax.all_gather(halves[1], "shard", axis=0, tiled=True),
-        lax.all_gather(halves[2], "shard", axis=1, tiled=True),
-    )
+    forward_set = gather_weights(sizes, *halves)
     block_out, saved = forward_pass(images, forward_set[0], forward_set[1], forward_set[2])
-    backward_set = (
-        lax.all_gather(halves[0], "shard", axis=0, tiled=True),
-        lax.all_gather(halves[1], "shard", axis=0, tiled=True),
-        lax.all_gather(halves[2], "shard", axis=1, tiled=True),
-    )
     input_grad, grad_down_local, grad_vectors_local, factors = backward_pass(
-        cotangent, saved, backward_set[0], backward_set[1], backward_set[2]
+        cotangent, saved, forward_set[0], forward_set[1], forward_set[2]
     )
     act_one, grad_proj, attended, hidden_half, act_two, up_half = factors
 
-    def column_part(activation, gradient):
-        return transposed_times(activation, gradient)
-
-    owned_in = lax.psum_scatter(
+    width = 4 * images.shape[2] // 2
+    attention_part = to_half(
         jnp.concatenate(
-            [
-                column_part(act_one, grad_proj),
-                column_part(attended, hidden_half),
-                column_part(act_two, up_half),
-            ],
-            axis=1,
-        ).astype(jnp.bfloat16),
-        "shard",
-        scatter_dimension=0,
-        tiled=True,
-    )
-    owned_down, owned_vectors = (
-        lax.psum_scatter(
-            grad_down_local.astype(jnp.bfloat16), "shard", scatter_dimension=0, tiled=True
-        ).astype(jnp.float32),
-        lax.psum_scatter(
-            grad_vectors_local.astype(jnp.bfloat16), "shard", scatter_dimension=1, tiled=True
-        ).astype(jnp.float32),
-    )
-    grad_in, grad_down, grad_vectors = (
-        lax.psum(owned_in, "rep").astype(jnp.float32),
-        lax.psum(owned_down.astype(jnp.bfloat16), "rep").astype(jnp.float32),
-        lax.psum(owned_vectors.astype(jnp.bfloat16), "rep").astype(jnp.float32),
+            [transposed_times(act_one, grad_proj), transposed_times(attended, hidden_half)], axis=1
+        )
+    )
+    up_part = to_half(transposed_times(act_two, up_half))
+    down_part = to_half(grad_down_local)
+    grad_down = reduce_matrix(sizes, down_part, "cxyz")
+    grad_in = jnp.concatenate(
+        [
+            reduce_matrix(sizes, attention_part[:, :width], "cyxz"),
+            reduce_matrix(sizes, attention_part[:, width:], "cxyz"),
+            reduce_matrix(sizes, up_part, "cyxz"),
+        ],
+        axis=1,
+    )
+    vector_sum = reduce_small(
+        sizes[0] * sizes[1] * sizes[2] * sizes[3],
+        to_half(grad_vectors_local).astype(jnp.float32),
+    )
+    owned = vectors.shape[1]
+    grad_vectors = lax.dynamic_slice_in_dim(
+        vector_sum, lax.axis_index("shard") * owned, owned, axis=1
     )
     new_in = adam_update(weights_in, mean_in, square_in, grad_in, RATE_MATRIX, DECAY_MATRIX)
     new_down = adam_update(
@@ -302,8 +566,9 @@
         P("shard", None),
         P(None, "shard"),
     )
+    sizes = grid_sizes(mesh.shape["shard"], mesh.shape["rep"])
     return jax.shard_map(
-        local,
+        functools.partial(local, sizes),
         mesh=mesh,
         in_specs=placed,
         out_specs=(

time: 624 us -> 318 us (0.51)
  waiting for transfers between devices: 481 us -> 87.6 us
  Pallas kernels: 0 us -> 72.8 us
  starting transfers between devices: 0.65 us -> 50.2 us
  blocking collectives: 38.9 us -> 0 us
  between operations: 14.6 us -> 1.61 us
  local copies, waits for them, and re-layouts: 13.3 us -> 25 us
    reduce_scatter x2 -> x0, waiting for transfers between devices: 215 us -> none  [the longest x1 165 us: local(): lax.psum_scatter(jnp.concatenate([column_part(act_one, grad_proj), column...]
    all_gather x2 -> x0, waiting for transfers between devices: 166 us -> none  [the longest x1 106 us: local(): lax.all_gather(halves[0], 'shard', axis=0, tiled=True)]
    ppermute x0 -> x41, waiting for transfers between devices: none -> 87.6 us  [the longest x24 70.5 us: scatter_axis(): got = lax.ppermute(take(lax.rem(me + k, size)), ('shard', 'rep'), shift(k))]
    pallas_call x0 -> x1, Pallas kernels: none -> 72.8 us  [gather_weights(): pl.pallas_call(body, name='gather_weights', out_shape=(jax.ShapeDtypeStru...]
    unnamed x7 -> x0, waiting for transfers between devices: 58.7 us -> none
    ppermute x0 -> x41, starting transfers between devices: none -> 50.2 us  [the longest x24 30.3 us: scatter_axis(): got = lax.ppermute(take(lax.rem(me + k, size)), ('shard', 'rep'), shift(k))]
    psum x1 -> x0, waiting for transfers between devices: 40.4 us -> none  [local(): lax.psum(owned_in, 'rep').astype(jnp.float32)]
    all_gather x1 -> x0, blocking collectives: 33.3 us -> none  [local(): lax.all_gather(halves[2], 'shard', axis=1, tiled=True)]
  transfers between devices with their start and end apart: 6 -> 41, of which waited for: 6 -> 19; matrix products, arithmetic and copies ran while one was open for 12% -> 20% of each run, Pallas kernels for 0% -> 0%
where the time goes in v1:
time: 318 us; the launch traced here: 317 us
  waiting for transfers between devices  87.6 us (28%)
  Pallas kernels  72.8 us (23%)
  matrix products  54.7 us (17%)
  starting transfers between devices  50.2 us (16%)
  local copies, waits for them, and re-layouts  25 us (8%)
  other arithmetic  25 us (8%)
    pallas_call x1, Pallas kernels, gather_weights(): pl.pallas_call(body, name='gather_weights', out_shape=(jax.ShapeDtypeStru...  72.8 us
    ppermute x24, waiting for transfers between devices, scatter_axis(): got = lax.ppermute(take(lax.rem(me + k, size)), ('shard', 'rep'), shift(k))  70.5 us
    ppermute x24, starting transfers between devices, scatter_axis(): got = lax.ppermute(take(lax.rem(me + k, size)), ('shard', 'rep'), shift(k))  30.3 us
    dot_general x4, matrix products, matmul(): return jnp.dot(left, right, preferred_element_type=jnp.float32)  14.8 us
    dot_general x4, matrix products, times_transposed(): lax.dot_general(left, right, (((1,), (1,)), ((), ())), preferred_element_...  13.3 us
    unnamed x69, local copies, waits for them, and re-layouts  12.5 us
    convert_element_type x16, other arithmetic, to_half(): return array_in.astype(jnp.bfloat16)  12.2 us
    dot_general x4, matrix products, transposed_times(): lax.dot_general(left, right, (((0,), (0,)), ((), ())), preferred_element_...  10.7 us
  transfers between devices with their start and end apart: 41, of which 19 were waited for; matrix products, arithmetic and copies ran while one was open for 20% of the time, Pallas kernels for 0%

profile of v1, /device:TPU:0, one launch (start us, length us, event | category | flops | bytes accessed | tf_op | source)
XLA Modules:
  0.0 317.0 jit_solution(17099199602392222069)
XLA Ops:
  2.7 72.8 %gather_weights.1 = (bf16[8,96,6144]{2,1,0:T(8,128)(2,1)S(1)}, bf16[8,4,96,768]{3,2,1,0:T(8,128)(2,1)S(1)}, bf16[8,12,96]{2,1,0:T(8,128)(2,1)S(1)}) custom-call(bf16[96,6144]{1,0:T(8,128)(2,1)S(1)} %convert_element_type.323.refs_0_, bf16[4,96,768]{2,1,0:T(8,128)(2,1)S(1)} %bitcast.243, bf16[12,96]{1,0:T(8,128)(2,1)S(1)} %convert_element_type.325.refs_2_), custom_call_target="tpu_custom_call" | custom-call | tf_op jit(solution)/shard_map/gather_weights/pallas_call | solution.py:397
  75.6 3.5 %copy-done = bf16[8,96,6144]{2,1,0:T(8,128)(2,1)} copy-done((bf16[8,96,6144]{2,1,0:T(8,128)(2,1)}, bf16[8,96,6144]{2,1,0:T(8,128)(2,1)S(1)}, u32[]{:S(2)}) %copy-start) | copy-done | bytes 9437208
  91.9 5.2 %multiply_convert_fusion.1 = (bf16[197,3072]{1,0:T(8,128)(2,1)}, f32[197,3072]{1,0:T(8,128)S(1)}) fusion(f32[3072]{0:T(1024)S(1)} %add.441, bf16[768,6144]{1,0:T(8,128)(2,1)} %bitcast.246, f32[197,768]{1,0:T(8,128)S(1)} %get-tuple-element.109, f32[768]{0:T(1024)S(1)} %add.438, f32[768]{0:T(1024)S(1)} %mul.265, f32[197]{0:T(256)S(1)} %add_rsqrt_fusion, ...), kind=kOutput, calls=%fused_computation.28 | convolution fusion | flops 933950208 | bytes 8974888 | tf_op jit(solution)/shard_map/dot_general | solution.py:29
  100.4 3.7 %convolution_convert_fusion.1 = bf16[768,3072]{1,0:T(8,128)(2,1)} fusion(bf16[197,3072]{1,0:T(8,128)(2,1)S(1)} %get-tuple-element.117, f32[197,768]{1,0:T(8,128)S(1)} %get-tuple-element.109, f32[768]{0:T(1024)S(1)} %add.438, f32[768]{0:T(1024)S(1)} %mul.265, f32[197]{0:T(256)S(1)} %add_rsqrt_fusion, f32[197]{0:T(256)S(1)} %broadcast_multiply_fusion.4), kind=kOutput, calls=%fused_computation.2 | convolution fusion | flops 932678400 | bytes 6541864 | tf_op jit(solution)/shard_map/dot_general | solution.py:39
  104.1 3.4 %dynamic-slice_bitcast_fusion.1 = bf16[4,2,2,24,3072]{4,3,2,1,0:T(8,128)(2,1)} fusion(bf16[4,2,2,2,24,3072]{5,4,3,2,1,0:T(8,128)(2,1)} %bitcast.258, s32[]{:T(128)S(6)} %select_n.153), kind=kLoop, calls=%fused_computation.45 | loop fusion | bytes 4718596 | tf_op jit(solution)/shard_map/jit(dynamic_index_in_dim)/squeeze | solution.py:446
  108.0 4.2 %multiply_reduce_fusion.2 = (bf16[768]{0:T(1024)(128)(2,1)S(1)}, f32[197]{0:T(256)S(1)}, f32[197]{0:T(256)S(1)}, bf16[768]{0:T(1024)(128)(2,1)S(1)}, f32[197,768]{1,0:T(8,128)S(1)}) fusion(f32[197,768]{1,0:T(8,128)S(1)} %get-tuple-element.109, f32[197]{0:T(256)S(1)} %add_rsqrt_fusion, f32[197]{0:T(256)S(1)} %broadcast_multiply_fusion.4, ...), kind=kOutput, calls=%fused_computation.107 | convolution fusion | flops 930922368 | bytes 7148624 | tf_op jit(solution)/shard_map/dot_general | solution.py:33
  122.5 4.5 %fusion.37 = bf16[12,64,197]{2,1,0:T(8,128)(2,1)} fusion(bf16[197,12,64]{0,2,1:T(8,128)(2,1)} %bitcast.274, f32[12,197,197]{1,2,0:T(8,128)} %fusion.123, f32[12,197,197]{1,2,0:T(8,128)S(1)} %get-tuple-element.107, f32[12,197]{1,0:T(8,128)S(1)} %log_add_fusion), kind=kOutput, calls=%fused_computation.55 | convolution fusion | flops 63955852 | bytes 4340304 | tf_op jit(solution)/shard_map/bhqk,bqhe->bkhe/dot_general | solution.py:171
  127.0 4.6 %fusion.118 = (bf16[12,64]{1,0:T(8,128)(2,1)S(1)}, bf16[1,197,12,64]{1,3,2,0:T(8,128)(2,1)}) fusion(bf16[197,12,64]{0,2,1:T(8,128)(2,1)} %bitcast.272, f32[12,197,197]{1,2,0:T(8,128)} %fusion.123, f32[12,197]{1,0:T(8,128)S(1)} %log_add_fusion, f32[12,197,197]{1,2,0:T(8,128)S(1)} %get-tuple-element.107), kind=kOutput, calls=%fused_computation.214 | convolution fusion | flops 64106380 | bytes 4341840 | tf_op jit(solution)/shard_map/bhqk,bkhe->bqhe/dot_general | solution.py:168
  138.8 4.2 %fusion.67 = (bf16[768]{0:T(1024)(128)(2,1)S(1)}, f32[197]{0:T(256)S(1)}, f32[197]{0:T(256)S(1)}, bf16[768]{0:T(1024)(128)(2,1)S(1)}, f32[197,768]{1,0:T(8,128)}) fusion(bf16[1,197,768]{2,1,0:T(8,128)(2,1)S(1)} %copy-done.10, f32[197]{0:T(256)S(1)} %add_rsqrt_fusion.1, f32[197]{0:T(256)S(1)} %broadcast_multiply_fusion.5, f32[768]{0:T(1024)S(1)} %mul.258, ...), kind=kOutput, calls=%fused_computation.100 | convolution fusion | flops 701406336 | bytes 5363792 | tf_op jit(solution)/shard_map/dot_general | solution.py:33
  144.4 3.0 convolution_convert_fusion
  151.4 4.7 %fusion.44 = bf16[1,197,768]{2,1,0:T(8,128)(2,1)} fusion(f32[197,768]{1,0:T(8,128)} %copy-done.5, bf16[197,3072]{1,0:T(8,128)(2,1)} %get-tuple-element.111, bf16[3072,768]{1,0:T(8,128)(2,1)} %bitcast.250, f32[768]{0:T(1024)S(1)} %add.447), kind=kOutput, calls=%fused_computation.63 | convolution fusion | flops 930016512 | bytes 6839808 | tf_op jit(solution)/shard_map/dot_general | solution.py:29
  161.0 3.5 %collective-permute-done.39 = f32[12,768]{1,0:T(8,128)S(1)} collective-permute-done((f32[12,768]{1,0:T(8,128)S(1)}, f32[12,768]{1,0:T(8,128)S(1)}, u32[]{:S(2)}, u32[]{:S(2)}) %collective-permute-start.39) | collective-permute-done | bytes 36896 | tf_op jit(solution)/shard_map/ppermute | solution.py:480
  164.5 7.4 %collective-permute-start.40 = (f32[12,768]{1,0:T(8,128)S(1)}, f32[12,768]{1,0:T(8,128)S(1)}, u32[]{:S(2)}, u32[]{:S(2)}) collective-permute-start(f32[12,768]{1,0:T(8,128)S(1)} %add.502), channel_id=1, source_target_pairs={{0,16},{1,17},{2,18},{3,19},{4,20},{5,21},{6,22},{7,23},{8,24},{9,... | collective-permute-start | bytes 110600 | tf_op jit(solution)/shard_map/ppermute | solution.py:480
  182.7 8.4 %collective-permute-done.10 = bf16[4,2,24,1536]{3,2,1,0:T(8,128)(2,1)S(1)} collective-permute-done((bf16[4,2,24,1536]{3,2,1,0:T(8,128)(2,1)S(1)}, bf16[4,2,24,1536]{3,2,1,0:T(8,128)(2,1)S(1)}, u32[]{:S(2)}, u32[]{:S(2)}) %collective-permute-start.10) | collective-permute-done | bytes 589856 | tf_op jit(solution)/shard_map/ppermute | solution.py:449
  192.9 3.8 %collective-permute-done.1 = bf16[4,2,24,1536]{3,2,1,0:T(8,128)(2,1)S(1)} collective-permute-done((bf16[4,2,24,1536]{3,2,1,0:T(8,128)(2,1)S(1)}, bf16[4,2,24,1536]{3,2,1,0:T(8,128)(2,1)S(1)}, u32[]{:S(2)}, u32[]{:S(2)}) %collective-permute-start.1) | collective-permute-done | bytes 589856 | tf_op jit(solution)/shard_map/ppermute | solution.py:449
  205.6 3.3 %collective-permute-start.5 = (bf16[24,1536]{1,0:T(8,128)(2,1)S(1)}, bf16[24,1536]{1,0:T(8,128)(2,1)S(1)}, u32[]{:S(2)}, u32[]{:S(2)}) collective-permute-start(bf16[24,1536]{1,0:T(8,128)(2,1)S(1)} %get-tuple-element.101), channel_id=1, source_target_pairs={{0,24},{1,25},{2,26},{3,27},{4,28},{5,29},{6,30},{7,31},{8,0},{9,1... | collective-permute-start | bytes 221192 | tf_op jit(solution)/shard_map/ppermute | solution.py:449
  211.7 4.6 %collective-permute-done.4 = bf16[24,1536]{1,0:T(8,128)(2,1)S(1)} collective-permute-done((bf16[24,1536]{1,0:T(8,128)(2,1)S(1)}, bf16[24,1536]{1,0:T(8,128)(2,1)S(1)}, u32[]{:S(2)}, u32[]{:S(2)}) %collective-permute-start.4) | collective-permute-done | bytes 73760 | tf_op jit(solution)/shard_map/ppermute | solution.py:449
  218.5 3.7 %collective-permute-done.6 = bf16[24,1536]{1,0:T(8,128)(2,1)S(1)} collective-permute-done((bf16[24,1536]{1,0:T(8,128)(2,1)S(1)}, bf16[24,1536]{1,0:T(8,128)(2,1)S(1)}, u32[]{:S(2)}, u32[]{:S(2)}) %collective-permute-start.6) | collective-permute-done | bytes 73760 | tf_op jit(solution)/shard_map/ppermute | solution.py:469
  230.8 23.9 %collective-permute-done.19 = bf16[4,2,24,3072]{3,2,1,0:T(8,128)(2,1)S(1)} collective-permute-done((bf16[4,2,24,3072]{3,2,1,0:T(8,128)(2,1)S(1)}, bf16[4,2,24,3072]{3,2,1,0:T(8,128)(2,1)S(1)}, u32[]{:S(2)}, u32[]{:S(2)}) %collective-permute-start.19) | collective-permute-done | bytes 1179680 | tf_op jit(solution)/shard_map/ppermute | solution.py:449
  260.3 10.2 %collective-permute-done.20 = bf16[4,24,3072]{2,1,0:T(8,128)(2,1)S(1)} collective-permute-done((bf16[4,24,3072]{2,1,0:T(8,128)(2,1)S(1)}, bf16[4,24,3072]{2,1,0:T(8,128)(2,1)S(1)}, u32[]{:S(2)}, u32[]{:S(2)}) %collective-permute-start.20) | collective-permute-done | bytes 589856 | tf_op jit(solution)/shard_map/ppermute | solution.py:449
  279.0 4.3 %collective-permute-start.30 = (bf16[96,768]{1,0:T(8,128)(2,1)S(1)}, bf16[96,768]{1,0:T(8,128)(2,1)S(1)}, u32[]{:S(2)}, u32[]{:S(2)}) collective-permute-start(bf16[96,768]{1,0:T(8,128)(2,1)S(1)} %get-tuple-element.94), channel_id=1, source_target_pairs={{0,8},{1,9},{2,10},{3,11},{4,12},{5,13},{6,14},{7,15},{8,16},{9,17... | collective-permute-start | bytes 442376 | tf_op jit(solution)/shard_map/ppermute | solution.py:449
  283.3 9.5 %collective-permute-done.22 = bf16[24,3072]{1,0:T(8,128)(2,1)S(1)} collective-permute-done((bf16[24,3072]{1,0:T(8,128)(2,1)S(1)}, bf16[24,3072]{1,0:T(8,128)(2,1)S(1)}, u32[]{:S(2)}, u32[]{:S(2)}) %collective-permute-start.22) | collective-permute-done | bytes 147488 | tf_op jit(solution)/shard_map/ppermute | solution.py:449
  300.9 4.0 %collective-permute-done.33 = bf16[96,768]{1,0:T(8,128)(2,1)S(1)} collective-permute-done((bf16[96,768]{1,0:T(8,128)(2,1)S(1)}, bf16[96,768]{1,0:T(8,128)(2,1)S(1)}, u32[]{:S(2)}, u32[]{:S(2)}) %collective-permute-start.33) | collective-permute-done | bytes 147488 | tf_op jit(solution)/shard_map/ppermute | solution.py:469
  312.7 4.3 %multiply_subtract_fusion = (f32[96,6144]{1,0:T(8,128)}, f32[96,6144]{1,0:T(8,128)}, f32[96,6144]{1,0:T(8,128)}, f32[96,6144]{1,0:T(8,128)}) fusion(f32[96,6144]{1,0:T(8,128)S(1)} %copy-done.3, f32[96,6144]{1,0:T(8,128)S(1)} %copy-done.13, f32[96,6144]{1,0:T(8,128)S(1)} %copy-done.14, bf16[96,3072]{1,0:T(8,128)(2,1)S(1)} %bitcast.270, ...), kind=kLoop, calls=%fused_computation.42 | loop fusion | flops 12386304 | bytes 17694720 | tf_op jit(solution)/shard_map/sub | solution.py:208
  (254 shorter events, 110.6 us)
Async XLA Ops:
  107.5 116.1 %collective-permute-start.18 = (bf16[4,2,2,24,3072]{4,3,2,1,0:T(8,128)(2,1)}, bf16[4,2,2,24,3072]{4,3,2,1,0:T(8,128)(2,1)}, u32[]{:S(2)}, u32[]{:S(2)}) collective-permute-start(bf16[4,2,2,24,3072]{4,3,2,1,0:T(8,128)(2,1)} %dynamic-slice_bitcast_fusion.1), channel_id=1, source_target_pairs={{0,1},{1,0},{2,3},{3,2},{4,5},{5,4},{6,7},{7,6},{8,9},{9,8},{10,11... | collective-permute-start | bytes 7077896 | tf_op jit(solution)/shard_map/ppermute | solution.py:449
  137.1 39.1 %collective-permute-start.9 = (bf16[4,2,2,24,1536]{4,3,2,1,0:T(8,128)(2,1)}, bf16[4,2,2,24,1536]{4,3,2,1,0:T(8,128)(2,1)}, u32[]{:S(2)}, u32[]{:S(2)}) collective-permute-start(bf16[4,2,2,24,1536]{4,3,2,1,0:T(8,128)(2,1)} %dynamic-slice_bitcast_fusion.4), channel_id=1, source_target_pairs={{0,1},{1,0},{2,3},{3,2},{4,5},{5,4},{6,7},{7,6},{8,9},{9,8},{10,11... | collective-permute-start | bytes 3538952 | tf_op jit(solution)/shard_map/ppermute | solution.py:449
  138.3 41.0 %collective-permute-start = (bf16[4,2,2,24,1536]{4,3,2,1,0:T(8,128)(2,1)}, bf16[4,2,2,24,1536]{4,3,2,1,0:T(8,128)(2,1)}, u32[]{:S(2)}, u32[]{:S(2)}) collective-permute-start(bf16[4,2,2,24,1536]{4,3,2,1,0:T(8,128)(2,1)} %dynamic-slice_bitcast_fusion.5), channel_id=1, source_target_pairs={{0,1},{1,0},{2,3},{3,2},{4,5},{5,4},{6,7},{7,6},{8,9},{9,8},{10,11... | collective-permute-start | bytes 3538952 | tf_op jit(solution)/shard_map/ppermute | solution.py:449
  150.3 76.9 %collective-permute-start.27 = (bf16[4,2,2,96,768]{4,3,2,1,0:T(8,128)(2,1)}, bf16[4,2,2,96,768]{4,3,2,1,0:T(8,128)(2,1)}, u32[]{:S(2)}, u32[]{:S(2)}) collective-permute-start(bf16[4,2,2,96,768]{4,3,2,1,0:T(8,128)(2,1)} %dynamic-slice_bitcast_fusion), channel_id=1, source_target_pairs={{0,1},{1,0},{2,3},{3,2},{4,5},{5,4},{6,7},{7,6},{8,9},{9,8},{10,11... | collective-permute-start | bytes 7077896 | tf_op jit(solution)/shard_map/ppermute | solution.py:449
  164.5 11.0 %collective-permute-start.40 = (f32[12,768]{1,0:T(8,128)S(1)}, f32[12,768]{1,0:T(8,128)S(1)}, u32[]{:S(2)}, u32[]{:S(2)}) collective-permute-start(f32[12,768]{1,0:T(8,128)S(1)} %add.502), channel_id=1, source_target_pairs={{0,16},{1,17},{2,18},{3,19},{4,20},{5,21},{6,22},{7,23},{8,24},{9,... | collective-permute-start | bytes 110600 | tf_op jit(solution)/shard_map/ppermute | solution.py:480
  178.3 12.8 %collective-permute-start.10 = (bf16[4,2,24,1536]{3,2,1,0:T(8,128)(2,1)S(1)}, bf16[4,2,24,1536]{3,2,1,0:T(8,128)(2,1)S(1)}, u32[]{:S(2)}, u32[]{:S(2)}) collective-permute-start(bf16[4,2,24,1536]{3,2,1,0:T(8,128)(2,1)S(1)} %dynamic-slice_bitcast_fusion.8), channel_id=1, source_target_pairs={{0,4},{1,5},{2,6},{3,7},{4,0},{5,1},{6,2},{7,3},{8,12},{9,13},{10,... | collective-permute-start | bytes 1769480 | tf_op jit(solution)/shard_map/ppermute | solution.py:449
  181.1 15.6 %collective-permute-start.1 = (bf16[4,2,24,1536]{3,2,1,0:T(8,128)(2,1)S(1)}, bf16[4,2,24,1536]{3,2,1,0:T(8,128)(2,1)S(1)}, u32[]{:S(2)}, u32[]{:S(2)}) collective-permute-start(bf16[4,2,24,1536]{3,2,1,0:T(8,128)(2,1)S(1)} %dynamic-slice_bitcast_fusion.9), channel_id=1, source_target_pairs={{0,2},{1,3},{2,0},{3,1},{4,6},{5,7},{6,4},{7,5},{8,10},{9,11},{10,... | collective-permute-start | bytes 1769480 | tf_op jit(solution)/shard_map/ppermute | solution.py:449
  191.3 8.7 %collective-permute-start.11 = (bf16[4,24,1536]{2,1,0:T(8,128)(2,1)S(1)}, bf16[4,24,1536]{2,1,0:T(8,128)(2,1)S(1)}, u32[]{:S(2)}, u32[]{:S(2)}) collective-permute-start(bf16[4,24,1536]{2,1,0:T(8,128)(2,1)S(1)} %dynamic-slice_bitcast_fusion.10), channel_id=1, source_target_pairs={{0,2},{1,3},{2,0},{3,1},{4,6},{5,7},{6,4},{7,5},{8,10},{9,11},{10,... | collective-permute-start | bytes 884744 | tf_op jit(solution)/shard_map/ppermute | solution.py:449
  202.0 9.0 %collective-permute-start.13 = (bf16[24,1536]{1,0:T(8,128)(2,1)S(1)}, bf16[24,1536]{1,0:T(8,128)(2,1)S(1)}, u32[]{:S(2)}, u32[]{:S(2)}) collective-permute-start(bf16[24,1536]{1,0:T(8,128)(2,1)S(1)} %get-tuple-element.105), channel_id=1, source_target_pairs={{0,16},{1,17},{2,18},{3,19},{4,20},{5,21},{6,22},{7,23},{8,24},{9,... | collective-permute-start | bytes 221192 | tf_op jit(solution)/shard_map/ppermute | solution.py:449
  217.8 9.4 %collective-permute-start.17 = (bf16[24,1536]{1,0:T(8,128)(2,1)S(1)}, bf16[24,1536]{1,0:T(8,128)(2,1)S(1)}, u32[]{:S(2)}, u32[]{:S(2)}) collective-permute-start(bf16[24,1536]{1,0:T(8,128)(2,1)S(1)} %get-tuple-element.83), channel_id=1, source_target_pairs={{0,3},{1,0},{2,1},{3,2},{4,7},{5,4},{6,5},{7,6},{8,11},{9,8},{10,9... | collective-permute-start | bytes 221192 | tf_op jit(solution)/shard_map/ppermute | solution.py:469
  223.5 32.9 %collective-permute-start.8 = (bf16[24,1536]{1,0:T(8,128)(2,1)S(1)}, bf16[24,1536]{1,0:T(8,128)(2,1)S(1)}, u32[]{:S(2)}, u32[]{:S(2)}) collective-permute-start(bf16[24,1536]{1,0:T(8,128)(2,1)S(1)} %get-tuple-element.81), channel_id=1, source_target_pairs={{0,3},{1,0},{2,1},{3,2},{4,7},{5,4},{6,5},{7,6},{8,11},{9,8},{10,9... | collective-permute-start | bytes 221192 | tf_op jit(solution)/shard_map/ppermute | solution.py:469
  226.3 28.4 %collective-permute-start.19 = (bf16[4,2,24,3072]{3,2,1,0:T(8,128)(2,1)S(1)}, bf16[4,2,24,3072]{3,2,1,0:T(8,128)(2,1)S(1)}, u32[]{:S(2)}, u32[]{:S(2)}) collective-permute-start(bf16[4,2,24,3072]{3,2,1,0:T(8,128)(2,1)S(1)} %dynamic-slice_bitcast_fusion.3), channel_id=1, source_target_pairs={{0,2},{1,3},{2,0},{3,1},{4,6},{5,7},{6,4},{7,5},{8,10},{9,11},{10,... | collective-permute-start | bytes 3538952 | tf_op jit(solution)/shard_map/ppermute | solution.py:449
  229.7 28.5 %collective-permute-start.28 = (bf16[4,2,96,768]{3,2,1,0:T(8,128)(2,1)S(1)}, bf16[4,2,96,768]{3,2,1,0:T(8,128)(2,1)S(1)}, u32[]{:S(2)}, u32[]{:S(2)}) collective-permute-start(bf16[4,2,96,768]{3,2,1,0:T(8,128)(2,1)S(1)} %dynamic-slice_bitcast_fusion.2), channel_id=1, source_target_pairs={{0,4},{1,5},{2,6},{3,7},{4,0},{5,1},{6,2},{7,3},{8,12},{9,13},{10,... | collective-permute-start | bytes 3538952 | tf_op jit(solution)/shard_map/ppermute | solution.py:449
  255.2 15.3 %collective-permute-start.20 = (bf16[4,24,3072]{2,1,0:T(8,128)(2,1)S(1)}, bf16[4,24,3072]{2,1,0:T(8,128)(2,1)S(1)}, u32[]{:S(2)}, u32[]{:S(2)}) collective-permute-start(bf16[4,24,3072]{2,1,0:T(8,128)(2,1)S(1)} %dynamic-slice_bitcast_fusion.7), channel_id=1, source_target_pairs={{0,4},{1,5},{2,6},{3,7},{4,0},{5,1},{6,2},{7,3},{8,12},{9,13},{10,... | collective-permute-start | bytes 1769480 | tf_op jit(solution)/shard_map/ppermute | solution.py:449
  258.6 14.9 %collective-permute-start.29 = (bf16[4,96,768]{2,1,0:T(8,128)(2,1)S(1)}, bf16[4,96,768]{2,1,0:T(8,128)(2,1)S(1)}, u32[]{:S(2)}, u32[]{:S(2)}) collective-permute-start(bf16[4,96,768]{2,1,0:T(8,128)(2,1)S(1)} %dynamic-slice_bitcast_fusion.6), channel_id=1, source_target_pairs={{0,2},{1,3},{2,0},{3,1},{4,6},{5,7},{6,4},{7,5},{8,10},{9,11},{10,... | collective-permute-start | bytes 1769480 | tf_op jit(solution)/shard_map/ppermute | solution.py:449
  270.7 8.3 %collective-permute-start.23 = (bf16[24,3072]{1,0:T(8,128)(2,1)S(1)}, bf16[24,3072]{1,0:T(8,128)(2,1)S(1)}, u32[]{:S(2)}, u32[]{:S(2)}) collective-permute-start(bf16[24,3072]{1,0:T(8,128)(2,1)S(1)} %get-tuple-element.98), channel_id=1, source_target_pairs={{0,24},{1,25},{2,26},{3,27},{4,28},{5,29},{6,30},{7,31},{8,0},{9,1... | collective-permute-start | bytes 442376 | tf_op jit(solution)/shard_map/ppermute | solution.py:449
  271.1 21.7 %collective-permute-start.22 = (bf16[24,3072]{1,0:T(8,128)(2,1)S(1)}, bf16[24,3072]{1,0:T(8,128)(2,1)S(1)}, u32[]{:S(2)}, u32[]{:S(2)}) collective-permute-start(bf16[24,3072]{1,0:T(8,128)(2,1)S(1)} %get-tuple-element.99), channel_id=1, source_target_pairs={{0,16},{1,17},{2,18},{3,19},{4,20},{5,21},{6,22},{7,23},{8,24},{9,... | collective-permute-start | bytes 442376 | tf_op jit(solution)/shard_map/ppermute | solution.py:449
  272.4 20.5 %collective-permute-start.21 = (bf16[24,3072]{1,0:T(8,128)(2,1)S(1)}, bf16[24,3072]{1,0:T(8,128)(2,1)S(1)}, u32[]{:S(2)}, u32[]{:S(2)}) collective-permute-start(bf16[24,3072]{1,0:T(8,128)(2,1)S(1)} %get-tuple-element.97), channel_id=1, source_target_pairs={{0,8},{1,9},{2,10},{3,11},{4,12},{5,13},{6,14},{7,15},{8,16},{9,17... | collective-permute-start | bytes 442376 | tf_op jit(solution)/shard_map/ppermute | solution.py:449
  273.8 20.9 %collective-permute-start.32 = (bf16[96,768]{1,0:T(8,128)(2,1)S(1)}, bf16[96,768]{1,0:T(8,128)(2,1)S(1)}, u32[]{:S(2)}, u32[]{:S(2)}) collective-permute-start(bf16[96,768]{1,0:T(8,128)(2,1)S(1)} %get-tuple-element.95), channel_id=1, source_target_pairs={{0,24},{1,25},{2,26},{3,27},{4,28},{5,29},{6,30},{7,31},{8,0},{9,1... | collective-permute-start | bytes 442376 | tf_op jit(solution)/shard_map/ppermute | solution.py:449
  276.5 20.7 %collective-permute-start.31 = (bf16[96,768]{1,0:T(8,128)(2,1)S(1)}, bf16[96,768]{1,0:T(8,128)(2,1)S(1)}, u32[]{:S(2)}, u32[]{:S(2)}) collective-permute-start(bf16[96,768]{1,0:T(8,128)(2,1)S(1)} %get-tuple-element.96), channel_id=1, source_target_pairs={{0,16},{1,17},{2,18},{3,19},{4,20},{5,21},{6,22},{7,23},{8,24},{9,... | collective-permute-start | bytes 442376 | tf_op jit(solution)/shard_map/ppermute | solution.py:449
  279.0 18.2 %collective-permute-start.30 = (bf16[96,768]{1,0:T(8,128)(2,1)S(1)}, bf16[96,768]{1,0:T(8,128)(2,1)S(1)}, u32[]{:S(2)}, u32[]{:S(2)}) collective-permute-start(bf16[96,768]{1,0:T(8,128)(2,1)S(1)} %get-tuple-element.94), channel_id=1, source_target_pairs={{0,8},{1,9},{2,10},{3,11},{4,12},{5,13},{6,14},{7,15},{8,16},{9,17... | collective-permute-start | bytes 442376 | tf_op jit(solution)/shard_map/ppermute | solution.py:449
  294.8 15.8 %collective-permute-start.26 = (bf16[24,3072]{1,0:T(8,128)(2,1)S(1)}, bf16[24,3072]{1,0:T(8,128)(2,1)S(1)}, u32[]{:S(2)}, u32[]{:S(2)}) collective-permute-start(bf16[24,3072]{1,0:T(8,128)(2,1)S(1)} %get-tuple-element.85), channel_id=1, source_target_pairs={{0,3},{1,0},{2,1},{3,2},{4,7},{5,4},{6,5},{7,6},{8,11},{9,8},{10,9... | collective-permute-start | bytes 442376 | tf_op jit(solution)/shard_map/ppermute | solution.py:469
  297.4 8.8 %collective-permute-start.34 = (bf16[96,768]{1,0:T(8,128)(2,1)S(1)}, bf16[96,768]{1,0:T(8,128)(2,1)S(1)}, u32[]{:S(2)}, u32[]{:S(2)}) collective-permute-start(bf16[96,768]{1,0:T(8,128)(2,1)S(1)} %get-tuple-element.79), channel_id=1, source_target_pairs={{0,2},{1,3},{2,0},{3,1},{4,6},{5,7},{6,4},{7,5},{8,10},{9,11},{10,... | collective-permute-start | bytes 442376 | tf_op jit(solution)/shard_map/ppermute | solution.py:469
  299.4 8.4 %collective-permute-start.35 = (bf16[96,768]{1,0:T(8,128)(2,1)S(1)}, bf16[96,768]{1,0:T(8,128)(2,1)S(1)}, u32[]{:S(2)}, u32[]{:S(2)}) collective-permute-start(bf16[96,768]{1,0:T(8,128)(2,1)S(1)} %get-tuple-element.79), channel_id=1, source_target_pairs={{0,3},{1,0},{2,1},{3,2},{4,7},{5,4},{6,5},{7,6},{8,11},{9,8},{10,9... | collective-permute-start | bytes 442376 | tf_op jit(solution)/shard_map/ppermute | solution.py:469
  (51 other events, 526.9 us)

commit v2 on v1

--- a/solution.py
+++ b/solution.py
@@ -416,6 +416,216 @@
     )
 
 
+def reduce_body(sizes, orders, *refs):
+    nz, nx, ny, nc = sizes
+    shards, reps = nz * nx, ny * nc
+    count = len(orders)
+    s = lax.axis_index("shard")
+    r = lax.axis_index("rep")
+    place = {"z": s // nx, "x": s % nx, "y": r // nc, "c": r % nc}
+    extent = {"z": nz, "x": nx, "y": ny, "c": nc}
+    parts, vec = refs[:count], refs[count]
+    outs, out_vec = refs[count + 1 : 2 * count + 1], refs[2 * count + 1]
+    bufs = refs[2 * count + 2 : 6 * count + 2]
+    vec_in, vec_sum, vec_rep = refs[6 * count + 2 : 6 * count + 5]
+    send_sem, recv_sem, rep_send, rep_recv, vs_send, vs_recv, vr_send, vr_recv = refs[
+        6 * count + 5 :
+    ]
+
+    def moved(name, k):
+        at = dict(place)
+        at[name] = lax.rem(at[name] + k, extent[name])
+        return (at["z"] * nx + at["x"], at["y"] * nc + at["c"])
+
+    barrier = pltpu.get_barrier_semaphore()
+    peers = [(lax.rem(s + k, shards), r) for k in range(1, shards)]
+    peers += [(s, lax.rem(r + k, reps)) for k in range(1, reps)]
+    for ps, pr in peers:
+        pl.semaphore_signal(
+            barrier,
+            inc=1,
+            device_id={"shard": ps, "rep": pr},
+            device_id_type=pl.DeviceIdType.MESH,
+        )
+    pl.semaphore_wait(barrier, len(peers))
+    started = []
+
+    def send(src, dst, ssem, rsem, target):
+        copy = pltpu.make_async_remote_copy(
+            src_ref=src,
+            dst_ref=dst,
+            send_sem=ssem,
+            recv_sem=rsem,
+            device_id={"shard": target[0], "rep": target[1]},
+            device_id_type=pl.DeviceIdType.MESH,
+        )
+        copy.start()
+        started.append(copy)
+        return copy
+
+    def pick(ref, names, name, i):
+        return ref.at[tuple(i if n == name else slice(None) for n in names)]
+
+    flights = {}
+
+    def launch(stream, stage, src):
+        order = orders[stream]
+        name = order[stage]
+        names = [n for n in "zxyc" if n not in order[:stage]]
+        buf = bufs[4 * stream + stage]
+        flights[stream, stage] = []
+        for k in range(1, extent[name]):
+            theirs = lax.rem(place[name] + k, extent[name])
+            flights[stream, stage].append(
+                send(
+                    pick(src, names, name, theirs),
+                    buf.at[k - 1],
+                    send_sem.at[stream, stage, k],
+                    recv_sem.at[stream, stage, k],
+                    moved(name, k),
+                )
+            )
+
+    def collect(stream, stage, src, dst):
+        order = orders[stream]
+        name = order[stage]
+        names = [n for n in "zxyc" if n not in order[:stage]]
+        rest = [n for n in names if n != name]
+        buf = bufs[4 * stream + stage]
+        for copy in flights[stream, stage]:
+            copy.wait_recv()
+        trips = math.prod(extent[n] for n in rest)
+
+        def step(i, carry):
+            at, left = {}, i
+            for n in reversed(rest):
+                at[n] = left % extent[n]
+                left = left // extent[n]
+            at[name] = place[name]
+            index = tuple(at[n] for n in rest)
+            total = src[tuple(at[n] for n in names)].astype(jnp.float32)
+            for k in range(1, extent[name]):
+                total = total + buf[(k - 1,) + index].astype(jnp.float32)
+            dst[index] = total.astype(dst.dtype)
+            return carry
+
+        if rest:
+            lax.fori_loop(0, trips, step, 0)
+        else:
+            total = src[place[name]].astype(jnp.float32)
+            for k in range(1, extent[name]):
+                total = total + buf[k - 1].astype(jnp.float32)
+            dst[...] = total.astype(dst.dtype)
+
+    for stream in range(count):
+        launch(stream, 0, parts[stream])
+    vec_flights = [
+        send(
+            vec.at[lax.rem(s + k, shards)],
+            vec_in.at[k - 1],
+            vs_send.at[k],
+            vs_recv.at[k],
+            (lax.rem(s + k, shards), r),
+        )
+        for k in range(1, shards)
+    ]
+    for stage in range(3):
+        for stream in range(count):
+            src = parts[stream] if stage == 0 else bufs[4 * stream + stage - 1].at[0]
+            mine = bufs[4 * stream + stage].at[0]
+            collect(stream, stage, src, mine)
+            launch(stream, stage + 1, mine)
+    for copy in vec_flights:
+        copy.wait_recv()
+    total = vec[s]
+    for k in range(1, shards):
+        total = total + vec_in[k - 1]
+    vec_sum[...] = total
+    vec_flights = [
+        send(
+            vec_sum,
+            vec_rep.at[k - 1],
+            vr_send.at[k],
+            vr_recv.at[k],
+            (s, lax.rem(r + k, reps)),
+        )
+        for k in range(1, reps)
+    ]
+    last = []
+    for stream in range(count):
+        mine = outs[stream].at[r]
+        collect(stream, 3, bufs[4 * stream + 2].at[0], mine)
+        for k in range(1, reps):
+            last.append(
+                send(
+                    mine,
+                    mine,
+                    rep_send.at[stream, k],
+                    rep_recv.at[stream, k],
+                    (s, lax.rem(r + k, reps)),
+                )
+            )
+    for copy in vec_flights:
+        copy.wait_recv()
+    total = vec_sum[...]
+    for k in range(1, reps):
+        total = total + vec_rep[k - 1]
+    out_vec[...] = total
+    for copy in last:
+        copy.wait_recv()
+    for copy in started:
+        copy.wait_send()
+
+
+def reduce_grads(sizes, parts, vec):
+    nz, nx, ny, nc = sizes
+    extent = {"z": nz, "x": nx, "y": ny, "c": nc}
+    shards, reps = nz * nx, ny * nc
+    orders = ["cyxz" if i % 2 == 0 else "cxyz" for i in range(len(parts))]
+    views, bufs, outs = [], [], []
+    for part, order in zip(parts, orders):
+        unit, cols = part.shape[0] // (shards * reps), part.shape[1]
+        views.append(part.reshape(nz, nx, ny, nc, unit, cols))
+        for stage in range(4):
+            rest = tuple(extent[n] for n in "zxyc" if n not in order[: stage + 1])
+            slots = max(1, extent[order[stage]] - 1)
+            bufs.append(pltpu.VMEM((slots,) + rest + (unit, cols), part.dtype))
+        outs.append(jax.ShapeDtypeStruct((reps, unit, cols), part.dtype))
+    most = max(sizes)
+    dma = pltpu.SemaphoreType.DMA
+    tile = vec.shape[1:]
+    count = len(parts)
+
+    def body(*refs):
+        reduce_body(sizes, orders, *refs)
+
+    results = pl.pallas_call(
+        body,
+        name="reduce_grads",
+        out_shape=tuple(outs) + (jax.ShapeDtypeStruct(tile, vec.dtype),),
+        in_specs=[pl.BlockSpec(memory_space=pltpu.VMEM)] * (count + 1),
+        out_specs=[pl.BlockSpec(memory_space=pltpu.VMEM)] * (count + 1),
+        scratch_shapes=bufs
+        + [
+            pltpu.VMEM((max(1, shards - 1),) + tile, vec.dtype),
+            pltpu.VMEM(tile, vec.dtype),
+            pltpu.VMEM((max(1, reps - 1),) + tile, vec.dtype),
+            dma((count, 4, most)),
+            dma((count, 4, most)),
+            dma((count, reps)),
+            dma((count, reps)),
+            dma((shards,)),
+            dma((shards,)),
+            dma((reps,)),
+            dma((reps,)),
+        ],
+        compiler_params=pltpu.CompilerParams(
+            collective_id=1, has_side_effects=True, vmem_limit_bytes=56 << 20
+        ),
+    )(*views, vec)
+    return ([out.reshape(-1, out.shape[2]) for out in results[:count]], results[count])
+
+
 def axis_info(sizes, name):
     nz, nx, ny, nc = sizes
     s = lax.axis_index("shard")
@@ -504,31 +714,38 @@
     )
     act_one, grad_proj, attended, hidden_half, act_two, up_half = factors
 
-    width = 4 * images.shape[2] // 2
+    down_part = to_half(grad_down_local)
+    up_part = to_half(transposed_times(act_two, up_half))
     attention_part = to_half(
         jnp.concatenate(
             [transposed_times(act_one, grad_proj), transposed_times(attended, hidden_half)], axis=1
         )
     )
-    up_part = to_half(transposed_times(act_two, up_half))
-    down_part = to_half(grad_down_local)
-    grad_down = reduce_matrix(sizes, down_part, "cxyz")
-    grad_in = jnp.concatenate(
-        [
-            reduce_matrix(sizes, attention_part[:, :width], "cyxz"),
-            reduce_matrix(sizes, attention_part[:, width:], "cxyz"),
-            reduce_matrix(sizes, up_part, "cyxz"),
-        ],
-        axis=1,
-    )
-    vector_sum = reduce_small(
-        sizes[0] * sizes[1] * sizes[2] * sizes[3],
-        to_half(grad_vectors_local).astype(jnp.float32),
-    )
+    parts = []
+    for part in (up_part, down_part, attention_part):
+        half = part.shape[1] // 2
+        parts += [part[:, :half], part[:, half:]]
+    shards, reps = sizes[0] * sizes[1], sizes[2] * sizes[3]
     owned = vectors.shape[1]
-    grad_vectors = lax.dynamic_slice_in_dim(
-        vector_sum, lax.axis_index("shard") * owned, owned, axis=1
-    )
+    small = to_half(grad_vectors_local).astype(jnp.float32)
+    if weights_in.shape[0] % (8 * reps) == 0 and weights_down.shape[0] % (8 * reps) == 0:
+        rows = vectors.shape[0]
+        tiles = jnp.swapaxes(small.reshape(rows, shards, owned), 0, 1)
+        tiles = jnp.pad(tiles, ((0, 0), (0, -rows % 8), (0, -owned % 128)))
+        sums, vector_sum = reduce_grads(sizes, parts, tiles)
+        sums = [part.astype(jnp.float32) for part in sums]
+        grad_vectors = vector_sum[:rows, :owned]
+    else:
+        sums = [
+            reduce_matrix(sizes, part, "cyxz" if i % 2 == 0 else "cxyz")
+            for i, part in enumerate(parts)
+        ]
+        vector_sum = reduce_small(shards * reps, small)
+        grad_vectors = lax.dynamic_slice_in_dim(
+            vector_sum, lax.axis_index("shard") * owned, owned, axis=1
+        )
+    grad_in = jnp.concatenate(sums[4:] + sums[:2], axis=1)
+    grad_down = jnp.concatenate(sums[2:4], axis=1)
     new_in = adam_update(weights_in, mean_in, square_in, grad_in, RATE_MATRIX, DECAY_MATRIX)
     new_down = adam_update(
         weights_down, mean_down, square_down, grad_down, RATE_MATRIX, DECAY_MATRIX

time: 318 us -> 273 us (0.86)
  Pallas kernels: 72.8 us -> 183 us
  waiting for transfers between devices: 87.6 us -> 0 us
  starting transfers between devices: 50.2 us -> 0 us
  matrix products: 54.7 us -> 47.8 us
  local copies, waits for them, and re-layouts: 25 us -> 18.7 us
  other arithmetic: 25 us -> 20.9 us
    pallas_call x0 -> x1, Pallas kernels: none -> 111 us  [reduce_grads(): pl.pallas_call(body, name='reduce_grads', out_shape=tuple(outs) + (jax.Sh...]
    ppermute x41 -> x0, waiting for transfers between devices: 87.6 us -> none  [the longest x24 70.5 us: scatter_axis(): got = lax.ppermute(take(lax.rem(me + k, size)), ('shard', 'rep'), shift(k))]
    ppermute x41 -> x0, starting transfers between devices: 50.2 us -> none  [the longest x24 30.3 us: scatter_axis(): got = lax.ppermute(take(lax.rem(me + k, size)), ('shard', 'rep'), shift(k))]
    convert_element_type x16 -> x4, other arithmetic: 12.2 us -> 2.25 us  [to_half(): return array_in.astype(jnp.bfloat16)]
    squeeze x16 -> x0, local copies, waits for them, and re-layouts: 8 us -> none  [scatter_axis(): take = lambda i: lax.dynamic_index_in_dim(value, i, dim, keepdims=False)]
    slice x0 -> x2, local copies, waits for them, and re-layouts: none -> 5.14 us  [local(): parts += [part[:, :half], part[:, half:]]]
    dot_general x4, matrix products: 14.8 us -> 10.5 us  [matmul(): return jnp.dot(left, right, preferred_element_type=jnp.float32)]
    unnamed x69 -> x71, local copies, waits for them, and re-layouts: 12.5 us -> 8.8 us
  transfers between devices with their start and end apart: 41 -> 0, of which waited for: 19 -> 0; matrix products, arithmetic and copies ran while one was open for 20% -> 0% of each run, Pallas kernels for 0% -> 0%
where the time goes in v2:
time: 273 us; the launch traced here: 272 us
  Pallas kernels  183 us (67%)
  matrix products  47.8 us (18%)
  other arithmetic  20.9 us (8%)
  local copies, waits for them, and re-layouts  18.7 us (7%)
    pallas_call x1, Pallas kernels, reduce_grads(): pl.pallas_call(body, name='reduce_grads', out_shape=tuple(outs) + (jax.Sh...  111 us
    pallas_call x1, Pallas kernels, gather_weights(): pl.pallas_call(body, name='gather_weights', out_shape=(jax.ShapeDtypeStru...  72.8 us
    dot_general x4, matrix products, times_transposed(): lax.dot_general(left, right, (((1,), (1,)), ((), ())), preferred_element_...  14.6 us
    dot_general x4, matrix products, matmul(): return jnp.dot(left, right, preferred_element_type=jnp.float32)  10.5 us
    sub x3, other arithmetic, adam_update(): weights - rate * (corr_first / (jnp.sqrt(corr_second) + ADAM_EPS) + decay...  9.49 us
    unnamed x71, local copies, waits for them, and re-layouts  8.8 us
    dot_general x4, matrix products, transposed_times(): lax.dot_general(left, right, (((0,), (0,)), ((), ())), preferred_element_...  7.16 us

profile of v2, /device:TPU:0, one launch (start us, length us, event | category | flops | bytes accessed | tf_op | source)
XLA Modules:
  0.0 272.1 jit_solution(10229481141128695575)
XLA Ops:
  6.4 72.8 %gather_weights.1 = (bf16[8,96,6144]{2,1,0:T(8,128)(2,1)S(1)}, bf16[8,4,96,768]{3,2,1,0:T(8,128)(2,1)S(1)}, bf16[8,12,96]{2,1,0:T(8,128)(2,1)S(1)}) custom-call(bf16[96,6144]{1,0:T(8,128)(2,1)S(1)} %convert_element_type.115.refs_0_, bf16[4,96,768]{2,1,0:T(8,128)(2,1)S(1)} %bitcast.113, bf16[12,96]{1,0:T(8,128)(2,1)S(1)} %convert_element_type.117.refs_2_), custom_call_target="tpu_custom_call" | custom-call | tf_op jit(solution)/shard_map/gather_weights/pallas_call | solution.py:397
  79.3 3.6 %copy-done = bf16[8,96,6144]{2,1,0:T(8,128)(2,1)} copy-done((bf16[8,96,6144]{2,1,0:T(8,128)(2,1)}, bf16[8,96,6144]{2,1,0:T(8,128)(2,1)S(1)}, u32[]{:S(2)}) %copy-start) | copy-done | bytes 9437208
  82.9 2.2 copy-done.1
  85.9 3.0 %fusion.11 = f32[197,2304]{1,0:T(8,128)S(1)} fusion(bf16[768,6144]{1,0:T(8,128)(2,1)} %bitcast.114, bf16[1,197,768]{2,1,0:T(8,128)(2,1)S(1)} %copy-done.11, f32[768]{0:T(1024)S(1)} %add.163, f32[768]{0:T(1024)S(1)} %mul.255, f32[197]{0:T(256)S(1)} %add_rsqrt_fusion.1, f32[197]{0:T(256)S(1)} %broadcast_multiply_fusion.5), kind=kOutput, calls=%fused_computation.15 | convolution fusion | flops 698079744 | bytes 5664808 | tf_op jit(solution)/shard_map/dot_general | solution.py:29
  93.0 1.9 fusion.90
  95.3 3.6 %multiply_convert_fusion.1 = (bf16[197,3072]{1,0:T(8,128)(2,1)S(1)}, f32[197,3072]{1,0:T(8,128)S(1)}) fusion(f32[3072]{0:T(1024)S(1)} %add.181, bf16[768,6144]{1,0:T(8,128)(2,1)} %bitcast.116, f32[197,768]{1,0:T(8,128)S(1)} %get-tuple-element.107, f32[768]{0:T(1024)S(1)} %add.178, f32[768]{0:T(1024)S(1)} %mul.262, f32[197]{0:T(256)S(1)} %add_rsqrt_fusion, ...), kind=kOutput, calls=%fused_computation.24 | convolution fusion | flops 933950208 | bytes 8974888 | tf_op jit(solution)/shard_map/dot_general | solution.py:29
  99.0 2.9 %fusion.93 = (bf16[3072]{0:T(1024)(128)(2,1)S(1)}, bf16[197,3072]{1,0:T(8,128)(2,1)}) fusion(f32[197,3072]{1,0:T(8,128)S(1)} %get-tuple-element.110, bf16[3072,768]{1,0:T(8,128)(2,1)S(1)} %bitcast.122, bf16[1,197,768]{2,1,0:T(8,128)(2,1)S(1)} %copy-done.14), kind=kOutput, calls=%fused_computation.134 | convolution fusion | flops 936216576 | bytes 8658432 | tf_op jit(solution)/shard_map/dot_general | solution.py:33
  102.0 1.9 fusion.38
  103.9 5.3 %multiply_reduce_fusion.2 = (bf16[768]{0:T(1024)(128)(2,1)S(1)}, f32[197]{0:T(256)S(1)}, f32[197]{0:T(256)S(1)}, bf16[768]{0:T(1024)(128)(2,1)S(1)}, f32[197,768]{1,0:T(8,128)}) fusion(f32[197,768]{1,0:T(8,128)S(1)} %get-tuple-element.107, f32[197]{0:T(256)S(1)} %add_rsqrt_fusion, f32[197]{0:T(256)S(1)} %broadcast_multiply_fusion.4, f32[768]{0:T(1024)S(1)} %mul.262, ...), kind=kOutput, calls=%fused_computation.81 | convolution fusion | flops 930922368 | bytes 7167056 | tf_op jit(solution)/shard_map/dot_general | solution.py:33
  111.1 2.5 convolution_convert_fusion.5
  113.6 1.9 copy.44
  115.5 2.4 fusion.88
  118.0 2.5 convolution_convert_fusion.3
  120.5 2.0 fusion.94
  122.5 4.5 %fusion.31 = bf16[12,64,197]{2,1,0:T(8,128)(2,1)} fusion(bf16[197,12,64]{0,2,1:T(8,128)(2,1)} %bitcast.137, f32[12,197,197]{1,2,0:T(8,128)} %fusion.94, f32[12,197,197]{1,2,0:T(8,128)S(1)} %get-tuple-element.105, f32[12,197]{1,0:T(8,128)S(1)} %log_add_fusion), kind=kOutput, calls=%fused_computation.41 | convolution fusion | flops 63955852 | bytes 4340304 | tf_op jit(solution)/shard_map/bhqk,bqhe->bkhe/dot_general | solution.py:171
  127.0 4.6 %fusion.89 = (bf16[12,64]{1,0:T(8,128)(2,1)S(1)}, bf16[1,197,12,64]{1,3,2,0:T(8,128)(2,1)}) fusion(bf16[197,12,64]{0,2,1:T(8,128)(2,1)} %bitcast.135, f32[12,197,197]{1,2,0:T(8,128)} %fusion.94, f32[12,197]{1,0:T(8,128)S(1)} %log_add_fusion, f32[12,197,197]{1,2,0:T(8,128)S(1)} %get-tuple-element.105), kind=kOutput, calls=%fused_computation.132 | convolution fusion | flops 64106380 | bytes 4341840 | tf_op jit(solution)/shard_map/bhqk,bkhe->bqhe/dot_general | solution.py:168
  131.6 3.9 %fusion.57 = (bf16[768]{0:T(1024)(128)(2,1)S(1)}, f32[197]{0:T(256)S(1)}, f32[197]{0:T(256)S(1)}, bf16[768]{0:T(1024)(128)(2,1)S(1)}, f32[197,768]{1,0:T(8,128)S(1)}) fusion(bf16[1,197,768]{2,1,0:T(8,128)(2,1)S(1)} %copy-done.13, f32[197]{0:T(256)S(1)} %add_rsqrt_fusion.1, f32[197]{0:T(256)S(1)} %broadcast_multiply_fusion.5, f32[768]{0:T(1024)S(1)} %mul.255, ...), kind=kOutput, calls=%fused_computation.74 | convolution fusion | flops 701406336 | bytes 5635664 | tf_op jit(solution)/shard_map/dot_general | solution.py:33
  139.6 2.5 pad_maximum_fusion
  142.1 1.8 convolution_convert_fusion.1
  143.9 2.5 fusion.87
  147.9 2.7 fusion.86
  150.6 110.6 %reduce_grads.1 = (bf16[4,24,1536]{2,1,0:T(8,128)(2,1)}, bf16[4,24,1536]{2,1,0:T(8,128)(2,1)}, bf16[4,96,384]{2,1,0:T(8,128)(2,1)}, bf16[4,96,384]{2,1,0:T(8,128...) custom-call(bf16[4,2,2,2,24,1536]{5,4,3,2,1,0:T(8,128)(2,1)} %bitcast.127, ...), custom_call_target="tpu_custom_call" | custom-call | tf_op jit(solution)/shard_map/reduce_grads/pallas_call | solution.py:602
  262.7 3.9 %multiply_subtract_fusion.1 = (f32[384,768]{1,0:T(8,128)}, f32[384,768]{1,0:T(8,128)}, f32[384,768]{1,0:T(8,128)}, f32[384,768]{1,0:T(8,128)}) fusion(f32[384,768]{1,0:T(8,128)S(1)} %copy-done.6, f32[384,768]{1,0:T(8,128)S(1)} %copy-done.21, f32[384,768]{1,0:T(8,128)S(1)} %copy-done.22, bf16[384,384]{1,0:T(8,128)(2,1)} %bitcast.143, ...), kind=kLoop, calls=%fused_computation.53 | loop fusion | flops 5603328 | bytes 8847360 | tf_op jit(solution)/shard_map/sub | solution.py:208
  267.8 4.3 %multiply_subtract_fusion = (f32[96,6144]{1,0:T(8,128)}, f32[96,6144]{1,0:T(8,128)}, f32[96,6144]{1,0:T(8,128)}, f32[96,6144]{1,0:T(8,128)}) fusion(f32[96,6144]{1,0:T(8,128)S(1)} %copy-done.3, f32[96,6144]{1,0:T(8,128)S(1)} %copy-done.16, f32[96,6144]{1,0:T(8,128)S(1)} %copy-done.17, bf16[96,1536]{1,0:T(8,128)(2,1)S(1)} %bitcast.145, ...), kind=kLoop, calls=%fused_computation.30 | loop fusion | flops 13565952 | bytes 17694720 | tf_op jit(solution)/shard_map/sub | solution.py:208
  (124 shorter events, 21.1 us)
Async XLA Ops:
  0.6 5.6 %copy-start.2 = (f32[96,6144]{1,0:T(8,128)S(1)}, f32[96,6144]{1,0:T(8,128)}, u32[]{:S(2)}) copy-start(f32[96,6144]{1,0:T(8,128)} %param.13) | copy-start | bytes 7077892
  6.3 79.6 %copy-start.11 = (bf16[1,197,768]{2,1,0:T(8,128)(2,1)S(1)}, bf16[1,197,768]{2,1,0:T(8,128)(2,1)}, u32[]{:S(2)}) copy-start(bf16[1,197,768]{2,1,0:T(8,128)(2,1)} %param.11) | copy-start | bytes 907780
  79.3 3.6 %copy-start = (bf16[8,96,6144]{2,1,0:T(8,128)(2,1)}, bf16[8,96,6144]{2,1,0:T(8,128)(2,1)S(1)}, u32[]{:S(2)}) copy-start(bf16[8,96,6144]{2,1,0:T(8,128)(2,1)S(1)} %get-tuple-element.25) | copy-start | bytes 28311556
  95.0 9.0 %copy-start.4 = (f32[197,768]{1,0:T(8,128)}, f32[197,768]{1,0:T(8,128)S(1)}, u32[]{:S(2)}) copy-start(f32[197,768]{1,0:T(8,128)S(1)} %get-tuple-element.107) | copy-start | bytes 1815556
  95.0 3.9 %slice-start = ((s8[4718592]{0:T(1024)(128)(4,1)}), s8[4194304]{0:T(1024)(128)(4,1)S(1)}, s32[]{:S(2)}) async-start(s8[4718592]{0:T(1024)(128)(4,1)} %bitcast.120), calls=%async_computation | async-start | bytes 8388608
  95.2 3.7 %slice-start.1 = ((s8[4718592]{0:T(1024)(128)(4,1)}), s8[524288]{0:T(1024)(128)(4,1)S(1)}, s32[]{:S(2)}) async-start(s8[4718592]{0:T(1024)(128)(4,1)} %bitcast.120), calls=%async_computation.1 | async-start | bytes 1048576
  95.3 3.8 %copy-start.14 = (bf16[1,197,768]{2,1,0:T(8,128)(2,1)S(1)}, bf16[1,197,768]{2,1,0:T(8,128)(2,1)}, u32[]{:S(2)}) copy-start(bf16[1,197,768]{2,1,0:T(8,128)(2,1)} %param.12) | copy-start | bytes 907780
  98.9 3.0 %copy-start.9 = (bf16[197,3072]{1,0:T(8,128)(2,1)}, bf16[197,3072]{1,0:T(8,128)(2,1)S(1)}, u32[]{:S(2)}) copy-start(bf16[197,3072]{1,0:T(8,128)(2,1)S(1)} %get-tuple-element.109) | copy-start | bytes 3631108
  127.0 4.6 %copy-start.13 = (bf16[1,197,768]{2,1,0:T(8,128)(2,1)S(1)}, bf16[1,197,768]{2,1,0:T(8,128)(2,1)}, u32[]{:S(2)}) copy-start(bf16[1,197,768]{2,1,0:T(8,128)(2,1)} %param.11) | copy-start | bytes 907780
  135.5 2.7 copy-start.23
  135.5 2.7 copy-start.31
  150.6 110.7 %copy-start.28 = (f32[12,96]{1,0:T(8,128)S(1)}, f32[12,96]{1,0:T(8,128)}, u32[]{:S(2)}) copy-start(f32[12,96]{1,0:T(8,128)} %param.15) | copy-start | bytes 13828
  150.6 110.7 %copy-start.29 = (f32[12,96]{1,0:T(8,128)S(1)}, f32[12,96]{1,0:T(8,128)}, u32[]{:S(2)}) copy-start(f32[12,96]{1,0:T(8,128)} %param.18) | copy-start | bytes 13828
  150.6 110.7 %copy-start.30 = (f32[12,96]{1,0:T(8,128)S(1)}, f32[12,96]{1,0:T(8,128)}, u32[]{:S(2)}) copy-start(f32[12,96]{1,0:T(8,128)} %param.21) | copy-start | bytes 13828
  150.6 112.0 %copy-start.6 = (f32[384,768]{1,0:T(8,128)S(1)}, f32[384,768]{1,0:T(8,128)}, u32[]{:S(2)}) copy-start(f32[384,768]{1,0:T(8,128)} %param.14) | copy-start | bytes 3538948
  150.6 112.0 %copy-start.21 = (f32[384,768]{1,0:T(8,128)S(1)}, f32[384,768]{1,0:T(8,128)}, u32[]{:S(2)}) copy-start(f32[384,768]{1,0:T(8,128)} %param.17) | copy-start | bytes 3538948
  150.6 112.0 %copy-start.22 = (f32[384,768]{1,0:T(8,128)S(1)}, f32[384,768]{1,0:T(8,128)}, u32[]{:S(2)}) copy-start(f32[384,768]{1,0:T(8,128)} %param.20) | copy-start | bytes 3538948
  262.6 3.9 %copy-start.3 = (f32[96,6144]{1,0:T(8,128)S(1)}, f32[96,6144]{1,0:T(8,128)}, u32[]{:S(2)}) copy-start(f32[96,6144]{1,0:T(8,128)} %param.13) | copy-start | bytes 7077892
  262.6 3.9 %copy-start.16 = (f32[96,6144]{1,0:T(8,128)S(1)}, f32[96,6144]{1,0:T(8,128)}, u32[]{:S(2)}) copy-start(f32[96,6144]{1,0:T(8,128)} %param.16) | copy-start | bytes 7077892
  262.6 5.0 %copy-start.17 = (f32[96,6144]{1,0:T(8,128)S(1)}, f32[96,6144]{1,0:T(8,128)}, u32[]{:S(2)}) copy-start(f32[96,6144]{1,0:T(8,128)} %param.19) | copy-start | bytes 7077892
  262.6 4.9 %copy-start.24 = (bf16[4,24,1536]{2,1,0:T(8,128)(2,1)S(1)}, bf16[4,24,1536]{2,1,0:T(8,128)(2,1)}, u32[]{:S(2)}) copy-start(bf16[4,24,1536]{2,1,0:T(8,128)(2,1)} %get-tuple-element.29) | copy-start | bytes 884740
  262.7 5.0 %copy-start.25 = (bf16[4,24,1536]{2,1,0:T(8,128)(2,1)S(1)}, bf16[4,24,1536]{2,1,0:T(8,128)(2,1)}, u32[]{:S(2)}) copy-start(bf16[4,24,1536]{2,1,0:T(8,128)(2,1)} %get-tuple-element.30) | copy-start | bytes 884740
  262.7 5.0 %copy-start.26 = (bf16[4,24,1536]{2,1,0:T(8,128)(2,1)S(1)}, bf16[4,24,1536]{2,1,0:T(8,128)(2,1)}, u32[]{:S(2)}) copy-start(bf16[4,24,1536]{2,1,0:T(8,128)(2,1)} %get-tuple-element.27) | copy-start | bytes 884740
  262.7 5.1 %copy-start.27 = (bf16[4,24,1536]{2,1,0:T(8,128)(2,1)S(1)}, bf16[4,24,1536]{2,1,0:T(8,128)(2,1)}, u32[]{:S(2)}) copy-start(bf16[4,24,1536]{2,1,0:T(8,128)(2,1)} %get-tuple-element.28) | copy-start | bytes 884740
  (11 other events, 24.4 us)

commit v3 on v2

--- a/solution.py
+++ b/solution.py
@@ -403,10 +403,10 @@
             jax.ShapeDtypeStruct((shards,) + vec.shape, vec.dtype),
         ),
         in_specs=[pl.BlockSpec(memory_space=pltpu.VMEM)] * 3,
-        out_specs=[pl.BlockSpec(memory_space=pl.ANY)] * 3,
+        out_specs=[pl.BlockSpec(memory_space=pltpu.HBM)] * 3,
         scratch_shapes=[dma((3,)), dma((shards,)), dma((shards,))] + sems,
         compiler_params=pltpu.CompilerParams(
-            collective_id=0, has_side_effects=True, vmem_limit_bytes=16 << 20
+            collective_id=0, has_side_effects=True, vmem_limit_bytes=56 << 20
         ),
     )(win, wdn.reshape(reps, rows_dn // reps, cols_dn), vec)
     return (
@@ -416,20 +416,29 @@
     )
 
 
-def reduce_body(sizes, orders, *refs):
+def reduce_body(sizes, streams, arrays, *refs):
     nz, nx, ny, nc = sizes
     shards, reps = nz * nx, ny * nc
-    count = len(orders)
+    count = len(streams)
+    orders = [order for _, _, _, order in streams]
     s = lax.axis_index("shard")
     r = lax.axis_index("rep")
     place = {"z": s // nx, "x": s % nx, "y": r // nc, "c": r % nc}
     extent = {"z": nz, "x": nx, "y": ny, "c": nc}
-    parts, vec = refs[:count], refs[count]
-    outs, out_vec = refs[count + 1 : 2 * count + 1], refs[2 * count + 1]
-    bufs = refs[2 * count + 2 : 6 * count + 2]
-    vec_in, vec_sum, vec_rep = refs[6 * count + 2 : 6 * count + 5]
+    vec = refs[arrays]
+    wholes, out_vec = refs[arrays + 1 : 2 * arrays + 1], refs[2 * arrays + 1]
+    parts = [
+        refs[array].at[(slice(None),) * 5 + (pl.ds(start, width),)]
+        for array, start, width, _ in streams
+    ]
+    outs = [
+        wholes[array].at[:, :, pl.ds(start, width)] for array, start, width, _ in streams
+    ]
+    base = 2 * arrays + 2
+    bufs = refs[base : base + 4 * count]
+    vec_in, vec_sum, vec_rep = refs[base + 4 * count : base + 4 * count + 3]
     send_sem, recv_sem, rep_send, rep_recv, vs_send, vs_recv, vr_send, vr_recv = refs[
-        6 * count + 5 :
+        base + 4 * count + 3 :
     ]
 
     def moved(name, k):
@@ -529,49 +538,84 @@
         )
         for k in range(1, shards)
     ]
-    for stage in range(3):
-        for stream in range(count):
-            src = parts[stream] if stage == 0 else bufs[4 * stream + stage - 1].at[0]
-            mine = bufs[4 * stream + stage].at[0]
-            collect(stream, stage, src, mine)
+    y, c = place["y"], place["c"]
+    across, to_core = {}, []
+
+    def advance(stream, stage):
+        src = parts[stream] if stage == 0 else bufs[4 * stream + stage - 1].at[0]
+        mine = bufs[4 * stream + stage].at[0] if stage < 3 else outs[stream].at[r]
+        collect(stream, stage, src, mine)
+        if stage < 3:
             launch(stream, stage + 1, mine)
-    for copy in vec_flights:
-        copy.wait_recv()
-    total = vec[s]
-    for k in range(1, shards):
-        total = total + vec_in[k - 1]
-    vec_sum[...] = total
-    vec_flights = [
-        send(
-            vec_sum,
-            vec_rep.at[k - 1],
-            vr_send.at[k],
-            vr_recv.at[k],
-            (s, lax.rem(r + k, reps)),
-        )
-        for k in range(1, reps)
-    ]
-    last = []
-    for stream in range(count):
-        mine = outs[stream].at[r]
-        collect(stream, 3, bufs[4 * stream + 2].at[0], mine)
-        for k in range(1, reps):
-            last.append(
+            return
+        for k in range(1, ny):
+            across[stream, k] = send(
+                mine,
+                mine,
+                rep_send.at[stream, k],
+                rep_recv.at[stream, k],
+                (s, lax.rem(y + k, ny) * nc + c),
+            )
+        share(stream, 0)
+
+    def share(stream, k):
+        unit = outs[stream].at[lax.rem(y + ny - k, ny) * nc + c]
+        for kc in range(1, nc):
+            slot = ny + k * nc + kc
+            to_core.append(
                 send(
-                    mine,
-                    mine,
-                    rep_send.at[stream, k],
-                    rep_recv.at[stream, k],
-                    (s, lax.rem(r + k, reps)),
+                    unit,
+                    unit,
+                    rep_send.at[stream, slot],
+                    rep_recv.at[stream, slot],
+                    (s, y * nc + lax.rem(c + kc, nc)),
                 )
             )
-    for copy in vec_flights:
+
+    def arrive(stream):
+        for k in range(1, ny):
+            across[stream, k].wait_recv()
+            share(stream, k)
+
+    def sum_vec():
+        for copy in vec_flights:
+            copy.wait_recv()
+        total = vec[s]
+        for k in range(1, shards):
+            total = total + vec_in[k - 1]
+        vec_sum[...] = total
+        return [
+            send(
+                vec_sum,
+                vec_rep.at[k - 1],
+                vr_send.at[k],
+                vr_recv.at[k],
+                (s, lax.rem(r + k, reps)),
+            )
+            for k in range(1, reps)
+        ]
+
+    lead = (0.0, 3.5, 7.0, 9.0, 11.0)
+    tasks = sorted(
+        (lead[stage] + stream * (1.0 if stage == 0 else 1.5), stage, stream)
+        for stage in range(5)
+        for stream in range(count)
+    )
+    spread = None
+    for _, stage, stream in tasks:
+        if stage < 4:
+            advance(stream, stage)
+        else:
+            arrive(stream)
+        if stage == 1 and stream == count - 1:
+            spread = sum_vec()
+    for copy in spread:
         copy.wait_recv()
     total = vec_sum[...]
     for k in range(1, reps):
         total = total + vec_rep[k - 1]
     out_vec[...] = total
-    for copy in last:
+    for copy in to_core:
         copy.wait_recv()
     for copy in started:
         copy.wait_send()
@@ -581,30 +625,34 @@
     nz, nx, ny, nc = sizes
     extent = {"z": nz, "x": nx, "y": ny, "c": nc}
     shards, reps = nz * nx, ny * nc
-    orders = ["cyxz" if i % 2 == 0 else "cxyz" for i in range(len(parts))]
-    views, bufs, outs = [], [], []
-    for part, order in zip(parts, orders):
+    views, bufs, outs, streams = [], [], [], []
+    for array, part in enumerate(parts):
         unit, cols = part.shape[0] // (shards * reps), part.shape[1]
         views.append(part.reshape(nz, nx, ny, nc, unit, cols))
-        for stage in range(4):
-            rest = tuple(extent[n] for n in "zxyc" if n not in order[: stage + 1])
-            slots = max(1, extent[order[stage]] - 1)
-            bufs.append(pltpu.VMEM((slots,) + rest + (unit, cols), part.dtype))
         outs.append(jax.ShapeDtypeStruct((reps, unit, cols), part.dtype))
+        pieces = 2 if cols % 256 == 0 and part.size >= 2 * min(part.shape) ** 2 else 1
+        for piece in range(pieces):
+            order = "cyxz" if pieces == 2 and piece == 0 else "cxyz"
+            width = cols // pieces
+            streams.append((array, piece * width, width, order))
+            for stage in range(4):
+                rest = tuple(extent[n] for n in "zxyc" if n not in order[: stage + 1])
+                slots = max(1, extent[order[stage]] - 1)
+                bufs.append(pltpu.VMEM((slots,) + rest + (unit, width), part.dtype))
     most = max(sizes)
     dma = pltpu.SemaphoreType.DMA
     tile = vec.shape[1:]
-    count = len(parts)
+    count, arrays = len(streams), len(parts)
 
     def body(*refs):
-        reduce_body(sizes, orders, *refs)
+        reduce_body(sizes, streams, arrays, *refs)
 
     results = pl.pallas_call(
         body,
         name="reduce_grads",
         out_shape=tuple(outs) + (jax.ShapeDtypeStruct(tile, vec.dtype),),
-        in_specs=[pl.BlockSpec(memory_space=pltpu.VMEM)] * (count + 1),
-        out_specs=[pl.BlockSpec(memory_space=pltpu.VMEM)] * (count + 1),
+        in_specs=[pl.BlockSpec(memory_space=pltpu.VMEM)] * (arrays + 1),
+        out_specs=[pl.BlockSpec(memory_space=pltpu.VMEM)] * (arrays + 1),
         scratch_shapes=bufs
         + [
             pltpu.VMEM((max(1, shards - 1),) + tile, vec.dtype),
@@ -612,8 +660,8 @@
             pltpu.VMEM((max(1, reps - 1),) + tile, vec.dtype),
             dma((count, 4, most)),
             dma((count, 4, most)),
-            dma((count, reps)),
-            dma((count, reps)),
+            dma((count, ny + reps)),
+            dma((count, ny + reps)),
             dma((shards,)),
             dma((shards,)),
             dma((reps,)),
@@ -623,7 +671,7 @@
             collective_id=1, has_side_effects=True, vmem_limit_bytes=56 << 20
         ),
     )(*views, vec)
-    return ([out.reshape(-1, out.shape[2]) for out in results[:count]], results[count])
+    return ([out.reshape(-1, out.shape[2]) for out in results[:arrays]], results[arrays])
 
 
 def axis_info(sizes, name):
@@ -716,15 +764,9 @@
 
     down_part = to_half(grad_down_local)
     up_part = to_half(transposed_times(act_two, up_half))
-    attention_part = to_half(
-        jnp.concatenate(
-            [transposed_times(act_one, grad_proj), transposed_times(attended, hidden_half)], axis=1
-        )
-    )
-    parts = []
-    for part in (up_part, down_part, attention_part):
-        half = part.shape[1] // 2
-        parts += [part[:, :half], part[:, half:]]
+    joint_part = to_half(transposed_times(act_one, grad_proj))
+    output_part = to_half(transposed_times(attended, hidden_half))
+    parts = [up_part, down_part, joint_part, output_part]
     shards, reps = sizes[0] * sizes[1], sizes[2] * sizes[3]
     owned = vectors.shape[1]
     small = to_half(grad_vectors_local).astype(jnp.float32)
@@ -744,8 +786,8 @@
         grad_vectors = lax.dynamic_slice_in_dim(
             vector_sum, lax.axis_index("shard") * owned, owned, axis=1
         )
-    grad_in = jnp.concatenate(sums[4:] + sums[:2], axis=1)
-    grad_down = jnp.concatenate(sums[2:4], axis=1)
+    grad_in = jnp.concatenate([sums[2], sums[3], sums[0]], axis=1)
+    grad_down = sums[1]
     new_in = adam_update(weights_in, mean_in, square_in, grad_in, RATE_MATRIX, DECAY_MATRIX)
     new_down = adam_update(
         weights_down, mean_down, square_down, grad_down, RATE_MATRIX, DECAY_MATRIX

time: 273 us -> 271 us (level)
  local copies, waits for them, and re-layouts: 18.7 us -> 7.73 us
  matrix products: 47.8 us -> 53.9 us
  Pallas kernels: 183 us -> 186 us
    dot_general x4, matrix products: 7.16 us -> 13.2 us  [transposed_times(): lax.dot_general(left, right, (((0,), (0,)), ((), ())), preferred_element_...]
    unnamed x71 -> x63, local copies, waits for them, and re-layouts: 8.8 us -> 2.93 us
    slice x2 -> x0, local copies, waits for them, and re-layouts: 5.14 us -> none  [local(): parts += [part[:, :half], part[:, half:]]]
where the time goes in v3:
time: 271 us; the launch traced here: 270 us
  Pallas kernels  186 us (69%)
  matrix products  53.9 us (20%)
  other arithmetic  21.6 us (8%)
  local copies, waits for them, and re-layouts  7.73 us (3%)
    pallas_call x1, Pallas kernels, reduce_grads(): pl.pallas_call(body, name='reduce_grads', out_shape=tuple(outs) + (jax.Sh...  111 us
    pallas_call x1, Pallas kernels, gather_weights(): pl.pallas_call(body, name='gather_weights', out_shape=(jax.ShapeDtypeStru...  75.3 us
    dot_general x4, matrix products, times_transposed(): lax.dot_general(left, right, (((1,), (1,)), ((), ())), preferred_element_...  14.6 us
    dot_general x4, matrix products, transposed_times(): lax.dot_general(left, right, (((0,), (0,)), ((), ())), preferred_element_...  13.2 us
    dot_general x4, matrix products, matmul(): return jnp.dot(left, right, preferred_element_type=jnp.float32)  10.5 us
    sub x3, other arithmetic, adam_update(): weights - rate * (corr_first / (jnp.sqrt(corr_second) + ADAM_EPS) + decay...  9.48 us

profile of v3, /device:TPU:0, one launch (start us, length us, event | category | flops | bytes accessed | tf_op | source)
XLA Modules:
  0.0 270.2 jit_solution(89139452244977973)
XLA Ops:
  5.5 2.1 convert_element_type.115
  8.8 75.3 %gather_weights.1 = (bf16[8,96,6144]{2,1,0:T(8,128)(2,1)}, bf16[8,4,96,768]{3,2,1,0:T(8,128)(2,1)}, bf16[8,12,96]{2,1,0:T(8,128)(2,1)}) custom-call(bf16[96,6144]{1,0:T(8,128)(2,1)} %convert_element_type.114.refs_0_, bf16[4,96,768]{2,1,0:T(8,128)(2,1)} %bitcast.120, bf16[12,96]{1,0:T(8,128)(2,1)} %convert_element_type.116.refs_2_), custom_call_target="tpu_custom_call" | custom-call | tf_op jit(solution)/shard_map/gather_weights/pallas_call | solution.py:397
  85.7 3.0 %fusion.11 = f32[197,2304]{1,0:T(8,128)S(1)} fusion(bf16[768,6144]{1,0:T(8,128)(2,1)} %bitcast.131, bf16[1,197,768]{2,1,0:T(8,128)(2,1)S(1)} %copy-done.8, f32[768]{0:T(1024)S(1)} %add.163, f32[768]{0:T(1024)S(1)} %mul.255, f32[197]{0:T(256)S(1)} %add_rsqrt_fusion.1, f32[197]{0:T(256)S(1)} %broadcast_multiply_fusion.5), kind=kOutput, calls=%fused_computation.15 | convolution fusion | flops 698079744 | bytes 5664808 | tf_op jit(solution)/shard_map/dot_general | solution.py:29
  90.1 1.5 multiply_reduce_fusion.1
  92.8 1.9 fusion.88
  95.0 3.6 %multiply_convert_fusion.1 = (bf16[197,3072]{1,0:T(8,128)(2,1)S(1)}, f32[197,3072]{1,0:T(8,128)S(1)}) fusion(f32[3072]{0:T(1024)S(1)} %add.181, bf16[768,6144]{1,0:T(8,128)(2,1)} %bitcast.133, f32[197,768]{1,0:T(8,128)S(1)} %get-tuple-element.97, f32[768]{0:T(1024)S(1)} %add.178, f32[768]{0:T(1024)S(1)} %mul.262, f32[197]{0:T(256)S(1)} %add_rsqrt_fusion, ...), kind=kOutput, calls=%fused_computation.24 | convolution fusion | flops 933950208 | bytes 8974888 | tf_op jit(solution)/shard_map/dot_general | solution.py:29
  98.8 2.9 %fusion.91 = (bf16[3072]{0:T(1024)(128)(2,1)S(1)}, bf16[197,3072]{1,0:T(8,128)(2,1)}) fusion(f32[197,3072]{1,0:T(8,128)S(1)} %get-tuple-element.100, bf16[3072,768]{1,0:T(8,128)(2,1)S(1)} %bitcast.141, bf16[1,197,768]{2,1,0:T(8,128)(2,1)S(1)} %copy-done.11), kind=kOutput, calls=%fused_computation.131 | convolution fusion | flops 936216576 | bytes 8658432 | tf_op jit(solution)/shard_map/dot_general | solution.py:33
  101.7 1.9 fusion.38
  103.7 5.3 %multiply_reduce_fusion.2 = (bf16[768]{0:T(1024)(128)(2,1)S(1)}, f32[197]{0:T(256)S(1)}, f32[197]{0:T(256)S(1)}, bf16[768]{0:T(1024)(128)(2,1)S(1)}, f32[197,768]{1,0:T(8,128)}) fusion(f32[197,768]{1,0:T(8,128)S(1)} %get-tuple-element.97, f32[197]{0:T(256)S(1)} %add_rsqrt_fusion, f32[197]{0:T(256)S(1)} %broadcast_multiply_fusion.4, f32[768]{0:T(1024)S(1)} %mul.262, ...), kind=kOutput, calls=%fused_computation.80 | convolution fusion | flops 930922368 | bytes 7167056 | tf_op jit(solution)/shard_map/dot_general | solution.py:33
  109.1 1.6 fusion.85
  110.8 2.5 convolution_convert_fusion.5
  113.4 1.9 copy.43
  115.3 2.4 fusion.86
  117.7 2.5 convolution_convert_fusion.3
  120.2 2.0 fusion.92
  122.2 4.5 %fusion.31 = bf16[12,64,197]{2,1,0:T(8,128)(2,1)} fusion(bf16[197,12,64]{0,2,1:T(8,128)(2,1)} %bitcast.124, f32[12,197,197]{1,2,0:T(8,128)} %fusion.92, f32[12,197,197]{1,2,0:T(8,128)S(1)} %get-tuple-element.95, f32[12,197]{1,0:T(8,128)S(1)} %log_add_fusion), kind=kOutput, calls=%fused_computation.40 | convolution fusion | flops 63955852 | bytes 4340304 | tf_op jit(solution)/shard_map/bhqk,bqhe->bkhe/dot_general | solution.py:171
  126.7 4.6 %fusion.87 = (bf16[12,64]{1,0:T(8,128)(2,1)S(1)}, bf16[1,197,12,64]{1,3,2,0:T(8,128)(2,1)}) fusion(bf16[197,12,64]{0,2,1:T(8,128)(2,1)} %bitcast.122, f32[12,197,197]{1,2,0:T(8,128)} %fusion.92, f32[12,197]{1,0:T(8,128)S(1)} %log_add_fusion, f32[12,197,197]{1,2,0:T(8,128)S(1)} %get-tuple-element.95), kind=kOutput, calls=%fused_computation.129 | convolution fusion | flops 64106380 | bytes 4341840 | tf_op jit(solution)/shard_map/bhqk,bkhe->bqhe/dot_general | solution.py:168
  131.3 3.9 %fusion.57 = (bf16[768]{0:T(1024)(128)(2,1)S(1)}, f32[197]{0:T(256)S(1)}, f32[197]{0:T(256)S(1)}, bf16[768]{0:T(1024)(128)(2,1)S(1)}, f32[197,768]{1,0:T(8,128)S(1)}) fusion(bf16[1,197,768]{2,1,0:T(8,128)(2,1)S(1)} %copy-done.10, f32[197]{0:T(256)S(1)} %add_rsqrt_fusion.1, f32[197]{0:T(256)S(1)} %broadcast_multiply_fusion.5, f32[768]{0:T(1024)S(1)} %mul.255, ...), kind=kOutput, calls=%fused_computation.73 | convolution fusion | flops 701406336 | bytes 5635664 | tf_op jit(solution)/shard_map/dot_general | solution.py:33
  138.0 3.1 %convolution_convert_fusion.2 = bf16[768,2304]{1,0:T(8,128)(2,1)} fusion(bf16[197,768]{0,1:T(8,128)(2,1)S(1)} %bitcast.130, bf16[197,768]{0,1:T(8,128)(2,1)S(1)} %bitcast.144, bf16[197,768]{0,1:T(8,128)(2,1)S(1)} %bitcast.146, bf16[1,197,768]{2,1,0:T(8,128)(2,1)S(1)} %copy-done.10, f32[768]{0:T(1024)S(1)} %add.163, f32[768]{0:T(1024)S(1)} %mul.255, ...), kind=kOutput, calls=%fused_computation.3 | convolution fusion | flops 702572544 | bytes 4757032 | tf_op jit(solution)/shard_map/dot_general | solution.py:39
  141.1 3.9 %convolution_convert_fusion.1 = bf16[768,3072]{1,0:T(8,128)(2,1)} fusion(bf16[197,3072]{1,0:T(8,128)(2,1)S(1)} %copy-done.17, f32[197,768]{1,0:T(8,128)S(1)} %copy-done.3, f32[768]{0:T(1024)S(1)} %add.178, f32[768]{0:T(1024)S(1)} %mul.262, f32[197]{0:T(256)S(1)} %add_rsqrt_fusion, f32[197]{0:T(256)S(1)} %broadcast_multiply_fusion.4), kind=kOutput, calls=%fused_computation.2 | convolution fusion | flops 932678400 | bytes 6541864 | tf_op jit(solution)/shard_map/dot_general | solution.py:39
  145.0 3.6 %convolution_convert_fusion = bf16[3072,768]{1,0:T(8,128)(2,1)} fusion(bf16[197,3072]{1,0:T(8,128)(2,1)S(1)} %copy-done.7, bf16[1,197,768]{2,1,0:T(8,128)(2,1)S(1)} %copy-done.12), kind=kOutput, calls=%fused_computation.1 | convolution fusion | flops 931921920 | bytes 6231552 | tf_op jit(solution)/shard_map/dot_general | solution.py:39
  148.7 110.6 %reduce_grads.1 = (bf16[4,24,3072]{2,1,0:T(8,128)(2,1)}, bf16[4,96,768]{2,1,0:T(8,128)(2,1)}, bf16[4,24,2304]{2,1,0:T(8,128)(2,1)}, bf16[4,24,768]{2,1,0:T(8,128)(2,1)}, f32[16,128]{1,0:T(8,128)}) custom-call(bf16[4,2,2,2,24,3072]{5,4,3,2,1,0:T(8,128)(2,1)} %bitcast.113, bf16[4,2,2,2,96,768]{5,4,3,2,1,0:T(8,128)(2,1)} %bitcast.112, ...), custom_call_target="tpu_custom_call" | custom-call | tf_op jit(solution)/shard_map/reduce_grads/pallas_call | solution.py:650
  260.8 3.9 %multiply_subtract_fusion.1 = (f32[384,768]{1,0:T(8,128)}, f32[384,768]{1,0:T(8,128)}, f32[384,768]{1,0:T(8,128)}, f32[384,768]{1,0:T(8,128)}) fusion(f32[384,768]{1,0:T(8,128)S(1)} %copy-done.4, f32[384,768]{1,0:T(8,128)S(1)} %copy-done.18, f32[384,768]{1,0:T(8,128)S(1)} %copy-done.19, bf16[4,96,768]{2,1,0:T(8,128)(2,1)} %get-tuple-element.28), kind=kLoop, calls=%fused_computation.52 | loop fusion | flops 4718592 | bytes 8847360 | tf_op jit(solution)/shard_map/sub | solution.py:208
  265.9 4.3 %multiply_subtract_fusion = (f32[96,6144]{1,0:T(8,128)}, f32[96,6144]{1,0:T(8,128)}, f32[96,6144]{1,0:T(8,128)}, f32[96,6144]{1,0:T(8,128)}) fusion(f32[96,6144]{1,0:T(8,128)S(1)} %copy-done.1, f32[96,6144]{1,0:T(8,128)S(1)} %copy-done.13, f32[96,6144]{1,0:T(8,128)S(1)} %copy-done.14, bf16[96,3072]{1,0:T(8,128)(2,1)S(1)} %bitcast.127, ...), kind=kLoop, calls=%fused_computation.29 | loop fusion | flops 12386304 | bytes 17694720 | tf_op jit(solution)/shard_map/sub | solution.py:208
  (113 shorter events, 16.1 us)
Async XLA Ops:
  0.6 7.0 %copy-start = (f32[96,6144]{1,0:T(8,128)S(1)}, f32[96,6144]{1,0:T(8,128)}, u32[]{:S(2)}) copy-start(f32[96,6144]{1,0:T(8,128)} %param.13) | copy-start | bytes 7077892
  7.7 78.0 %copy-start.8 = (bf16[1,197,768]{2,1,0:T(8,128)(2,1)S(1)}, bf16[1,197,768]{2,1,0:T(8,128)(2,1)}, u32[]{:S(2)}) copy-start(bf16[1,197,768]{2,1,0:T(8,128)(2,1)} %param.11) | copy-start | bytes 907780
  94.7 8.9 %copy-start.2 = (f32[197,768]{1,0:T(8,128)}, f32[197,768]{1,0:T(8,128)S(1)}, u32[]{:S(2)}) copy-start(f32[197,768]{1,0:T(8,128)S(1)} %get-tuple-element.97) | copy-start | bytes 1815556
  94.8 3.9 %slice-start = ((s8[4718592]{0:T(1024)(128)(4,1)}), s8[4194304]{0:T(1024)(128)(4,1)S(1)}, s32[]{:S(2)}) async-start(s8[4718592]{0:T(1024)(128)(4,1)} %bitcast.139), calls=%async_computation | async-start | bytes 8388608
  95.0 3.7 %copy-start.11 = (bf16[1,197,768]{2,1,0:T(8,128)(2,1)S(1)}, bf16[1,197,768]{2,1,0:T(8,128)(2,1)}, u32[]{:S(2)}) copy-start(bf16[1,197,768]{2,1,0:T(8,128)(2,1)} %param.12) | copy-start | bytes 907780
  95.0 3.8 %slice-start.1 = ((s8[4718592]{0:T(1024)(128)(4,1)}), s8[524288]{0:T(1024)(128)(4,1)S(1)}, s32[]{:S(2)}) async-start(s8[4718592]{0:T(1024)(128)(4,1)} %bitcast.139), calls=%async_computation.1 | async-start | bytes 1048576
  98.7 3.0 %copy-start.6 = (bf16[197,3072]{1,0:T(8,128)(2,1)}, bf16[197,3072]{1,0:T(8,128)(2,1)S(1)}, u32[]{:S(2)}) copy-start(bf16[197,3072]{1,0:T(8,128)(2,1)S(1)} %get-tuple-element.99) | copy-start | bytes 3631108
  126.7 4.6 %copy-start.10 = (bf16[1,197,768]{2,1,0:T(8,128)(2,1)S(1)}, bf16[1,197,768]{2,1,0:T(8,128)(2,1)}, u32[]{:S(2)}) copy-start(bf16[1,197,768]{2,1,0:T(8,128)(2,1)} %param.11) | copy-start | bytes 907780
  138.0 3.1 %copy-start.3 = (f32[197,768]{1,0:T(8,128)S(1)}, f32[197,768]{1,0:T(8,128)}, u32[]{:S(2)}) copy-start(f32[197,768]{1,0:T(8,128)} %copy-done.2) | copy-start | bytes 1815556
  138.0 3.1 %copy-start.17 = (bf16[197,3072]{1,0:T(8,128)(2,1)S(1)}, bf16[197,3072]{1,0:T(8,128)(2,1)}, u32[]{:S(2)}) copy-start(bf16[197,3072]{1,0:T(8,128)(2,1)} %get-tuple-element.105) | copy-start | bytes 3631108
  141.1 4.0 %copy-start.7 = (bf16[197,3072]{1,0:T(8,128)(2,1)S(1)}, bf16[197,3072]{1,0:T(8,128)(2,1)}, u32[]{:S(2)}) copy-start(bf16[197,3072]{1,0:T(8,128)(2,1)} %copy-done.6) | copy-start | bytes 3631108
  141.1 4.0 %copy-start.12 = (bf16[1,197,768]{2,1,0:T(8,128)(2,1)S(1)}, bf16[1,197,768]{2,1,0:T(8,128)(2,1)}, u32[]{:S(2)}) copy-start(bf16[1,197,768]{2,1,0:T(8,128)(2,1)} %param.12) | copy-start | bytes 907780
  148.7 110.7 %copy-start.24 = (f32[12,96]{1,0:T(8,128)S(1)}, f32[12,96]{1,0:T(8,128)}, u32[]{:S(2)}) copy-start(f32[12,96]{1,0:T(8,128)} %param.15) | copy-start | bytes 13828
  148.7 110.7 %copy-start.25 = (f32[12,96]{1,0:T(8,128)S(1)}, f32[12,96]{1,0:T(8,128)}, u32[]{:S(2)}) copy-start(f32[12,96]{1,0:T(8,128)} %param.18) | copy-start | bytes 13828
  148.7 110.7 %copy-start.26 = (f32[12,96]{1,0:T(8,128)S(1)}, f32[12,96]{1,0:T(8,128)}, u32[]{:S(2)}) copy-start(f32[12,96]{1,0:T(8,128)} %param.21) | copy-start | bytes 13828
  148.7 112.0 %copy-start.4 = (f32[384,768]{1,0:T(8,128)S(1)}, f32[384,768]{1,0:T(8,128)}, u32[]{:S(2)}) copy-start(f32[384,768]{1,0:T(8,128)} %param.14) | copy-start | bytes 3538948
  148.7 112.0 %copy-start.18 = (f32[384,768]{1,0:T(8,128)S(1)}, f32[384,768]{1,0:T(8,128)}, u32[]{:S(2)}) copy-start(f32[384,768]{1,0:T(8,128)} %param.17) | copy-start | bytes 3538948
  148.7 112.0 %copy-start.19 = (f32[384,768]{1,0:T(8,128)S(1)}, f32[384,768]{1,0:T(8,128)}, u32[]{:S(2)}) copy-start(f32[384,768]{1,0:T(8,128)} %param.20) | copy-start | bytes 3538948
  260.7 3.9 %copy-start.1 = (f32[96,6144]{1,0:T(8,128)S(1)}, f32[96,6144]{1,0:T(8,128)}, u32[]{:S(2)}) copy-start(f32[96,6144]{1,0:T(8,128)} %param.13) | copy-start | bytes 7077892
  260.7 3.9 %copy-start.13 = (f32[96,6144]{1,0:T(8,128)S(1)}, f32[96,6144]{1,0:T(8,128)}, u32[]{:S(2)}) copy-start(f32[96,6144]{1,0:T(8,128)} %param.16) | copy-start | bytes 7077892
  260.7 5.0 %copy-start.14 = (f32[96,6144]{1,0:T(8,128)S(1)}, f32[96,6144]{1,0:T(8,128)}, u32[]{:S(2)}) copy-start(f32[96,6144]{1,0:T(8,128)} %param.19) | copy-start | bytes 7077892
  260.8 5.0 %copy-start.20 = (bf16[4,24,3072]{2,1,0:T(8,128)(2,1)S(1)}, bf16[4,24,3072]{2,1,0:T(8,128)(2,1)}, u32[]{:S(2)}) copy-start(bf16[4,24,3072]{2,1,0:T(8,128)(2,1)} %get-tuple-element.27) | copy-start | bytes 1769476
  260.8 5.1 %copy-start.21 = (bf16[4,24,2304]{2,1,0:T(8,128)(2,1)S(1)}, bf16[4,24,2304]{2,1,0:T(8,128)(2,1)}, u32[]{:S(2)}) copy-start(bf16[4,24,2304]{2,1,0:T(8,128)(2,1)} %get-tuple-element.25) | copy-start | bytes 1327108
  260.8 5.1 %copy-start.23 = (bf16[4,24,768]{2,1,0:T(8,128)(2,1)S(1)}, bf16[4,24,768]{2,1,0:T(8,128)(2,1)}, u32[]{:S(2)}) copy-start(bf16[4,24,768]{2,1,0:T(8,128)(2,1)} %get-tuple-element.26) | copy-start | bytes 442372
  (7 other events, 16.3 us)
